TPU v7x, 32 devices: a whole 2x2x4 slice. The times are simulated.
32 devices in a mesh: grp: 2 (over y), row: 4 (over z), col: 2 (over x), frm: 2 (over core).
Axes of the slice: x: 2, y: 2, z: 4, core: 2. Of those that a mesh axis runs over, the one named last changes fastest.
Arguments:
- latent: bfloat16 [4, 16, 320, 256], P(('grp', 'frm'), 'row', 'col'), parts along dimension 0, may hold values from -6 to 6
- proj_weight: bfloat16 [256, 128], replicated, may hold values from -0.375 to 0.375
- proj_bias: float32 [128], replicated, may hold values from -3 to 3
- cache_one: bfloat16 [4, 32, 640, 128], P(('grp', 'frm'), 'row', 'col'), parts along dimension 0, may hold values from -6 to 6
- cache_two: bfloat16 [4, 32, 640, 128], P(('grp', 'frm'), 'row', 'col'), parts along dimension 0, may hold values from -6 to 6
- conv_one: bfloat16 [3, 3, 3, 128, 128], replicated, may hold values from -0.109375 to 0.109375
- bias_one: float32 [128], replicated, may hold values from -3 to 3
- conv_two: bfloat16 [3, 3, 3, 128, 128], replicated, may hold values from -0.109375 to 0.109375
- bias_two: float32 [128], replicated, may hold values from -3 to 3
Outputs:
- decoded: bfloat16 [4, 32, 640, 128], P(('grp', 'frm'), 'row', 'col'), parts along dimension 0
There are 2 independent parts, one for each index of `grp`. A program takes and returns all parts, laid end to end along the dimension named above; an argument that names none is the same for every part. Nothing has to cross between parts.
All inputs are finite; a program needn't handle non-finite values.
Results may differ from a plain program's by a relative error of at most 0.0044.
Values may be sent and summed in bfloat16 or wider, within the bound.
A program may use at most 64 MiB of HBM per device.

v0:
```python
import jax
import jax.numpy as jnp
from jax import lax
from jax.sharding import PartitionSpec as P


def padded_2(cells, sides, width):
    for axis, dim in sides:
        count = lax.axis_size(axis)
        ends = count - 1
        head = lax.slice_in_dim(cells, 0, width, axis=dim)
        tail = lax.slice_in_dim(cells, cells.shape[dim] - width, cells.shape[dim], axis=dim)
        cells = jnp.concatenate(
            [
                lax.ppermute(tail, axis, [(i, (i + 1) % count) for i in range(ends)]),
                cells,
                lax.ppermute(head, axis, [((i + 1) % count, i) for i in range(ends)]),
            ],
            axis=dim,
        )
    return cells


def from_partner(x, axis, stride):
    return lax.ppermute(x, axis, [(i, i ^ 1 << stride) for i in range(lax.axis_size(axis))])


def neighbour_frames(cached, current):
    leading = lax.axis_index("frm") == 0
    paired = jnp.stack([cached, current])
    rimmed = padded_2(paired, (("row", 1), ("col", 2)), 1)
    payload = jnp.where(leading, rimmed[1], rimmed[0])
    middle = from_partner(payload, "frm", 0)
    padded = jnp.stack([rimmed[0], middle, rimmed[1]])
    return padded


def causal_conv(padded, weight, bias):
    tile_rows, tile_cols, channels = (padded.shape[1] - 2, padded.shape[2] - 2, padded.shape[3])
    folded = weight.reshape(3, 3, 3 * channels, weight.shape[-1])
    summed = jnp.zeros((tile_rows * tile_cols, weight.shape[-1]), jnp.float32)
    for frame_step in range(3):
        for row_step in range(3):
            stencil = jnp.concatenate(
                [
                    padded[
                        frame_step, row_step : row_step + tile_rows, col_step : col_step + tile_cols
                    ]
                    for col_step in range(3)
                ],
                axis=-1,
            ).reshape(tile_rows * tile_cols, 3 * channels)
            summed = summed + jnp.dot(
                stencil, folded[frame_step, row_step], preferred_element_type=jnp.float32
            )
    return (summed + bias).reshape(tile_rows, tile_cols, -1)


def per_device(
    latent, proj_weight, proj_bias, cache_one, cache_two, conv_one, bias_one, conv_two, bias_two
):
    coarse = latent[0]
    half_rows, half_cols, widths = coarse.shape
    projected = (
        jnp.dot(
            coarse.reshape(half_rows * half_cols, widths),
            proj_weight,
            preferred_element_type=jnp.float32,
        )
        + proj_bias
    )
    projected = projected.reshape(half_rows, half_cols, -1).astype(jnp.bfloat16)
    upsampled = jnp.repeat(jnp.repeat(projected, 2, axis=0), 2, axis=1)
    act_one = jax.nn.silu(upsampled.astype(jnp.float32)).astype(jnp.bfloat16)
    first_out = causal_conv(neighbour_frames(cache_one[0], act_one), conv_one, bias_one)
    act_two = jax.nn.silu(first_out).astype(jnp.bfloat16)
    second_out = causal_conv(neighbour_frames(cache_two[0], act_two), conv_two, bias_two)
    decoded = (upsampled.astype(jnp.float32) + second_out).astype(jnp.bfloat16)
    return decoded[None]


def solution(mesh):
    placed = (
        P(("grp", "frm"), "row", "col", None),
        P(),
        P(),
        P(("grp", "frm"), "row", "col", None),
        P(("grp", "frm"), "row", "col", None),
        P(),
        P(),
        P(),
        P(),
    )
    return jax.shard_map(
        per_device,
        mesh=mesh,
        in_specs=placed,
        out_specs=P(("grp", "frm"), "row", "col", None),
        check_vma=False,
    )
```

profile of v0, /device:TPU:0, one launch (start us, length us, event | category | flops | bytes accessed | tf_op | source)
XLA Modules:
  0.0 66.7 jit_solution(3401604732000481537)
XLA Ops:
  0.0 1.0 %copy-done = bf16[1,4,160,256]{3,2,1,0:T(8,128)(2,1)S(1)} copy-done((bf16[1,4,160,256]{3,2,1,0:T(8,128)(2,1)S(1)}, bf16[1,4,160,256]{3,2,1,0:T(8,128)(2,1)}, u32[]{:S(2)}) %copy-start) | copy-done | bytes 327704
  1.0 1.1 %fusion.94 = bf16[640,128]{1,0:T(8,128)(2,1)S(1)} fusion(bf16[640,256]{1,0:T(8,128)(2,1)S(1)} %bitcast.126, bf16[256,128]{1,0:T(8,128)(2,1)} %param.10, f32[128]{0:T(128)} %param.11), kind=kOutput, calls=%fused_computation.122 | convolution fusion | flops 42106880 | bytes 557568 | tf_op jit(solution)/shard_map/dot_general | solution.py:65
  2.1 0.5 broadcast_in_dim.5
  3.2 1.3 %collective-permute-start.1 = (bf16[2,1,320,128]{3,2,1,0:T(8,128)(2,1)S(1)}, bf16[2,1,320,128]{3,2,1,0:T(8,128)(2,1)S(1)}, u32[]{:S(2)}, u32[]{:S(2)}) collective-permute-start(bf16[2,1,320,128]{3,2,1,0:T(8,128)(2,1)S(1)} %get-tuple-element.52), channel_id=1, source_target_pairs={{4,0},{8,4},{12,8},{5,1},{9,5},{13,9},{6,2},{10,6},{14,10},{7,3},{... | collective-permute-start | bytes 491528 | tf_op jit(solution)/shard_map/ppermute | solution.py:17
  4.5 5.6 %collective-permute-start = (bf16[2,1,320,128]{3,2,1,0:T(8,128)(2,1)S(1)}, bf16[2,1,320,128]{3,2,1,0:T(8,128)(2,1)S(1)}, u32[]{:S(2)}, u32[]{:S(2)}) collective-permute-start(bf16[2,1,320,128]{3,2,1,0:T(8,128)(2,1)S(1)} %get-tuple-element.51), channel_id=1, source_target_pairs={{0,4},{4,8},{8,12},{1,5},{5,9},{9,13},{2,6},{6,10},{10,14},{3,7},{... | collective-permute-start | bytes 491528 | tf_op jit(solution)/shard_map/ppermute | solution.py:15
  10.1 1.2 %multiply_convert_fusion.2 = bf16[2560,128]{1,0:T(8,128)(2,1)} fusion(f32[2560,128]{1,0:T(8,128)S(1)} %bitcast.130), kind=kLoop, calls=%fused_computation.119 | loop fusion | flops 1638400 | bytes 1966080 | tf_op jit(solution)/shard_map/convert_element_type | solution.py:74
  11.3 1.1 %collective-permute-done.1 = bf16[2,1,320,128]{3,2,1,0:T(8,128)(2,1)S(1)} collective-permute-done((bf16[2,1,320,128]{3,2,1,0:T(8,128)(2,1)S(1)}, bf16[2,1,320,128]{3,2,1,0:T(8,128)(2,1)S(1)}, u32[]{:S(2)}, u32[]{:S(2)}) %collective-permute-start.1) | collective-permute-done | bytes 163872 | tf_op jit(solution)/shard_map/ppermute | solution.py:17
  12.4 1.2 %collective-permute-done = bf16[2,1,320,128]{3,2,1,0:T(8,128)(2,1)S(1)} collective-permute-done((bf16[2,1,320,128]{3,2,1,0:T(8,128)(2,1)S(1)}, bf16[2,1,320,128]{3,2,1,0:T(8,128)(2,1)S(1)}, u32[]{:S(2)}, u32[]{:S(2)}) %collective-permute-start) | collective-permute-done | bytes 163872 | tf_op jit(solution)/shard_map/ppermute | solution.py:15
  13.6 3.6 %collective-permute-start.2 = (bf16[2,10,1,128]{3,2,1,0:T(2,128)(2,1)S(1)}, bf16[2,10,1,128]{3,2,1,0:T(2,128)(2,1)S(1)}, u32[]{:S(2)}, u32[]{:S(2)}) collective-permute-start(bf16[2,10,1,128]{3,2,1,0:T(2,128)(2,1)S(1)} %get-tuple-element.35), channel_id=1, source_target_pairs={{0,2},{1,3},{4,6},{5,7},{8,10},{9,11},{12,14},{13,15},{16,18},{17,... | collective-permute-start | bytes 15368 | tf_op jit(solution)/shard_map/ppermute | solution.py:15
  17.2 1.3 %collective-permute-start.3 = (bf16[2,10,1,128]{3,2,1,0:T(2,128)(2,1)S(1)}, bf16[2,10,1,128]{3,2,1,0:T(2,128)(2,1)S(1)}, u32[]{:S(2)}, u32[]{:S(2)}) collective-permute-start(bf16[2,10,1,128]{3,2,1,0:T(2,128)(2,1)S(1)} %get-tuple-element.36), channel_id=1, source_target_pairs={{2,0},{3,1},{6,4},{7,5},{10,8},{11,9},{14,12},{15,13},{18,16},{19,... | collective-permute-start | bytes 15368 | tf_op jit(solution)/shard_map/ppermute | solution.py:17
  18.8 3.9 %collective-permute-done.3 = bf16[2,10,1,128]{3,2,1,0:T(2,128)(2,1)S(1)} collective-permute-done((bf16[2,10,1,128]{3,2,1,0:T(2,128)(2,1)S(1)}, bf16[2,10,1,128]{3,2,1,0:T(2,128)(2,1)S(1)}, u32[]{:S(2)}, u32[]{:S(2)}) %collective-permute-start.3) | collective-permute-done | bytes 5152 | tf_op jit(solution)/shard_map/ppermute | solution.py:17
  22.7 0.6 pad_maximum_fusion.1
  23.5 1.7 %maximum_maximum_fusion = (bf16[2,10,321,128]{3,2,1,0:T(8,128)(2,1)S(1)}, bf16[2,10,321,128]{3,2,1,0:T(8,128)(2,1)S(1)}) fusion(bf16[2,1,320,128]{3,2,1,0:T(8,128)(2,1)S(1)} %collective-permute-done.1, bf16[1,8,320,128]{3,2,1,0:T(8,128)(2,1)S(1)} %multiply_convert_fusion.3, bf16[1,8,320,128]{3,2,1,0:T(8,128)(2,1)S(1)} %copy-done.2, ...), kind=kLoop, calls=%fused_computation.110 | loop fusion | flops 16435200 | bytes 4935680 | tf_op jit(solution)/shard_map/concatenate | solution.py:13
  25.2 1.4 %fusion.117 = (bf16[1,8,320,128]{3,2,1,0:T(8,128)(2,1)S(1)}, bf16[1,8,320,128]{3,2,1,0:T(8,128)(2,1)S(1)}, bf16[1,8,320,128]{3,2,1,0:T(8,128)(2,1)S(1)}, bf16[1,...) fusion(bf16[2,10,321,128]{3,2,1,0:T(8,128)(2,1)S(1)} %get-tuple, ...), kind=kLoop, calls=%fused_computation.189 | loop fusion | bytes 15728640 | tf_op jit(solution)/shard_map/slice | solution.py:46
  26.7 0.7 %fusion.2 = f32[2560,128]{1,0:T(8,128)S(1)} fusion(bf16[2560,128]{1,0:T(8,128)(2,1)S(1)} %bitcast.187, bf16[2560,128]{1,0:T(8,128)(2,1)S(1)} %bitcast.169, bf16[2560,128]{1,0:T(8,128)(2,1)S(1)} %bitcast.186, bf16[3,3,384,128]{3,2,1,0:T(8,128)(2,1)S(1)} %bitcast.188), kind=kOutput, calls=%fused_computation.18 | convolution fusion | flops 257556480 | bytes 3375104 | tf_op jit(solution)/shard_map/dot_general | solution.py:53
  27.4 0.7 %convolution_add_fusion.15 = f32[2560,128]{1,0:T(8,128)S(1)} fusion(f32[2560,128]{1,0:T(8,128)S(1)} %fusion.2, bf16[2560,128]{1,0:T(8,128)(2,1)S(1)} %bitcast.185, bf16[2560,128]{1,0:T(8,128)(2,1)S(1)} %bitcast.132, bf16[2560,128]{1,0:T(8,128)(2,1)S(1)} %bitcast.184, bf16[3,3,384,128]{3,2,1,0:T(8,128)(2,1)S(1)} %bitcast.189), kind=kOutput, calls=%fused_computation.15 | convolution fusion | flops 257884160 | bytes 4685824 | tf_op jit(solution)/shard_map/dot_general | solution.py:53
  28.1 0.7 %convolution_add_fusion.14 = f32[2560,128]{1,0:T(8,128)S(1)} fusion(f32[2560,128]{1,0:T(8,128)S(1)} %convolution_add_fusion.15, bf16[2560,128]{1,0:T(8,128)(2,1)S(1)} %bitcast.183, bf16[2560,128]{1,0:T(8,128)(2,1)S(1)} %bitcast.167, bf16[2560,128]{1,0:T(8,128)(2,1)S(1)} %bitcast.182, bf16[3,3,384,128]{3,2,1,0:T(8,128)(2,1)S(1)} %bitcast.190), kind=kOutput, calls=%fused_computation.14 | convolution fusion | flops 257884160 | bytes 4685824 | tf_op jit(solution)/shard_map/dot_general | solution.py:53
  28.8 1.1 %fusion.120 = (bf16[1,8,320,128]{3,2,1,0:T(8,128)(2,1)S(1)}, bf16[1,8,320,128]{3,2,1,0:T(8,128)(2,1)S(1)}, bf16[1,8,320,128]{3,2,1,0:T(8,128)(2,1)S(1)}, bf16[1,...) fusion(bf16[1,10,322,128]{3,2,1,0:T(8,128)(2,1)S(1)} %bitcast.127), kind=kLoop, calls=%fused_computation.192 | loop fusion | bytes 11796480 | tf_op jit(solution)/shard_map/slice | solution.py:46
  29.9 0.7 %convolution_add_fusion.13 = f32[2560,128]{1,0:T(8,128)S(1)} fusion(f32[2560,128]{1,0:T(8,128)S(1)} %convolution_add_fusion.14, bf16[2560,128]{1,0:T(8,128)(2,1)S(1)} %bitcast.149, bf16[2560,128]{1,0:T(8,128)(2,1)S(1)} %bitcast.150, bf16[2560,128]{1,0:T(8,128)(2,1)S(1)} %bitcast.151, bf16[3,3,384,128]{3,2,1,0:T(8,128)(2,1)S(1)} %bitcast.191), kind=kOutput, calls=%fused_computation.13 | convolution fusion | flops 257884160 | bytes 4685824 | tf_op jit(solution)/shard_map/dot_general | solution.py:53
  30.6 0.7 %convolution_add_fusion.12 = f32[2560,128]{1,0:T(8,128)S(1)} fusion(f32[2560,128]{1,0:T(8,128)S(1)} %convolution_add_fusion.13, bf16[2560,128]{1,0:T(8,128)(2,1)S(1)} %bitcast.143, bf16[2560,128]{1,0:T(8,128)(2,1)S(1)} %bitcast.144, bf16[2560,128]{1,0:T(8,128)(2,1)S(1)} %bitcast.145, bf16[3,3,384,128]{3,2,1,0:T(8,128)(2,1)S(1)} %bitcast.192), kind=kOutput, calls=%fused_computation.12 | convolution fusion | flops 257884160 | bytes 4685824 | tf_op jit(solution)/shard_map/dot_general | solution.py:53
  31.3 0.7 %convolution_add_fusion.11 = f32[2560,128]{1,0:T(8,128)S(1)} fusion(f32[2560,128]{1,0:T(8,128)S(1)} %convolution_add_fusion.12, bf16[2560,128]{1,0:T(8,128)(2,1)S(1)} %bitcast.138, bf16[2560,128]{1,0:T(8,128)(2,1)S(1)} %bitcast.139, bf16[2560,128]{1,0:T(8,128)(2,1)S(1)} %bitcast.137, bf16[3,3,384,128]{3,2,1,0:T(8,128)(2,1)S(1)} %bitcast.193), kind=kOutput, calls=%fused_computation.11 | convolution fusion | flops 257884160 | bytes 4685824 | tf_op jit(solution)/shard_map/dot_general | solution.py:53
  32.0 0.7 %convolution_add_fusion.10 = f32[2560,128]{1,0:T(8,128)S(1)} fusion(f32[2560,128]{1,0:T(8,128)S(1)} %convolution_add_fusion.11, bf16[2560,128]{1,0:T(8,128)(2,1)S(1)} %bitcast.181, bf16[2560,128]{1,0:T(8,128)(2,1)S(1)} %bitcast.159, bf16[2560,128]{1,0:T(8,128)(2,1)S(1)} %bitcast.180, bf16[3,3,384,128]{3,2,1,0:T(8,128)(2,1)S(1)} %bitcast.194), kind=kOutput, calls=%fused_computation.10 | convolution fusion | flops 257884160 | bytes 4685824 | tf_op jit(solution)/shard_map/dot_general | solution.py:53
  33.0 0.7 %convolution_add_fusion.9 = f32[2560,128]{1,0:T(8,128)S(1)} fusion(f32[2560,128]{1,0:T(8,128)S(1)} %convolution_add_fusion.10, bf16[2560,128]{1,0:T(8,128)(2,1)S(1)} %bitcast.179, bf16[2560,128]{1,0:T(8,128)(2,1)S(1)} %copy-done.4, bf16[2560,128]{1,0:T(8,128)(2,1)S(1)} %bitcast.178, bf16[3,3,384,128]{3,2,1,0:T(8,128)(2,1)S(1)} %bitcast.195), kind=kOutput, calls=%fused_computation.9 | convolution fusion | flops 257884160 | bytes 4685824 | tf_op jit(solution)/shard_map/dot_general | solution.py:53
  33.7 0.8 %multiply_convert_fusion = (bf16[2560,128]{1,0:T(8,128)(2,1)S(1)}, f32[2560,128]{1,0:T(8,128)S(1)}) fusion(f32[128]{0:T(128)S(1)} %copy-done.7, f32[2560,128]{1,0:T(8,128)S(1)} %convolution_add_fusion.9, bf16[3,3,384,128]{3,2,1,0:T(8,128)(2,1)S(1)} %bitcast.196, bf16[2560,128]{1,0:T(8,128)(2,1)S(1)} %bitcast.177, bf16[2560,128]{1,0:T(8,128)(2,1)S(1)} %bitcast.157, ...), kind=kOutput, calls=%fused_computation.117 | convolution fusion | flops 259850240 | bytes 5341696 | tf_op jit(solution)/shard_map/dot_general | solution.py:53
  34.9 0.7 %copy-done.3 = bf16[1,8,320,128]{3,2,1,0:T(8,128)(2,1)S(1)} copy-done((bf16[1,8,320,128]{3,2,1,0:T(8,128)(2,1)S(1)}, bf16[1,8,320,128]{3,2,1,0:T(8,128)(2,1)}, u32[]{:S(2)}) %copy-start.3) | copy-done | bytes 655384
  35.6 1.3 %collective-permute-start.6 = (bf16[2,1,320,128]{3,2,1,0:T(8,128)(2,1)S(1)}, bf16[2,1,320,128]{3,2,1,0:T(8,128)(2,1)S(1)}, u32[]{:S(2)}, u32[]{:S(2)}) collective-permute-start(bf16[2,1,320,128]{3,2,1,0:T(8,128)(2,1)S(1)} %get-tuple-element.48), channel_id=1, source_target_pairs={{4,0},{8,4},{12,8},{5,1},{9,5},{13,9},{6,2},{10,6},{14,10},{7,3},{... | collective-permute-start | bytes 491528 | tf_op jit(solution)/shard_map/ppermute | solution.py:17
  36.9 5.0 %collective-permute-start.5 = (bf16[2,1,320,128]{3,2,1,0:T(8,128)(2,1)S(1)}, bf16[2,1,320,128]{3,2,1,0:T(8,128)(2,1)S(1)}, u32[]{:S(2)}, u32[]{:S(2)}) collective-permute-start(bf16[2,1,320,128]{3,2,1,0:T(8,128)(2,1)S(1)} %get-tuple-element.47), channel_id=1, source_target_pairs={{0,4},{4,8},{8,12},{1,5},{5,9},{9,13},{2,6},{6,10},{10,14},{3,7},{... | collective-permute-start | bytes 491528 | tf_op jit(solution)/shard_map/ppermute | solution.py:15
  42.0 2.9 %collective-permute-done.6 = bf16[2,1,320,128]{3,2,1,0:T(8,128)(2,1)S(1)} collective-permute-done((bf16[2,1,320,128]{3,2,1,0:T(8,128)(2,1)S(1)}, bf16[2,1,320,128]{3,2,1,0:T(8,128)(2,1)S(1)}, u32[]{:S(2)}, u32[]{:S(2)}) %collective-permute-start.6) | collective-permute-done | bytes 163872 | tf_op jit(solution)/shard_map/ppermute | solution.py:17
  44.9 1.2 %collective-permute-done.5 = bf16[2,1,320,128]{3,2,1,0:T(8,128)(2,1)S(1)} collective-permute-done((bf16[2,1,320,128]{3,2,1,0:T(8,128)(2,1)S(1)}, bf16[2,1,320,128]{3,2,1,0:T(8,128)(2,1)S(1)}, u32[]{:S(2)}, u32[]{:S(2)}) %collective-permute-start.5) | collective-permute-done | bytes 163872 | tf_op jit(solution)/shard_map/ppermute | solution.py:15
  46.1 1.6 %collective-permute-start.7 = (bf16[2,10,1,128]{3,2,1,0:T(2,128)(2,1)S(1)}, bf16[2,10,1,128]{3,2,1,0:T(2,128)(2,1)S(1)}, u32[]{:S(2)}, u32[]{:S(2)}) collective-permute-start(bf16[2,10,1,128]{3,2,1,0:T(2,128)(2,1)S(1)} %get-tuple-element.31), channel_id=1, source_target_pairs={{0,2},{1,3},{4,6},{5,7},{8,10},{9,11},{12,14},{13,15},{16,18},{17,... | collective-permute-start | bytes 15368 | tf_op jit(solution)/shard_map/ppermute | solution.py:15
  47.7 1.5 %collective-permute-start.8 = (bf16[2,10,1,128]{3,2,1,0:T(2,128)(2,1)S(1)}, bf16[2,10,1,128]{3,2,1,0:T(2,128)(2,1)S(1)}, u32[]{:S(2)}, u32[]{:S(2)}) collective-permute-start(bf16[2,10,1,128]{3,2,1,0:T(2,128)(2,1)S(1)} %get-tuple-element.32), channel_id=1, source_target_pairs={{2,0},{3,1},{6,4},{7,5},{10,8},{11,9},{14,12},{15,13},{18,16},{19,... | collective-permute-start | bytes 15368 | tf_op jit(solution)/shard_map/ppermute | solution.py:17
  49.5 3.8 %collective-permute-done.8 = bf16[2,10,1,128]{3,2,1,0:T(2,128)(2,1)S(1)} collective-permute-done((bf16[2,10,1,128]{3,2,1,0:T(2,128)(2,1)S(1)}, bf16[2,10,1,128]{3,2,1,0:T(2,128)(2,1)S(1)}, u32[]{:S(2)}, u32[]{:S(2)}) %collective-permute-start.8) | collective-permute-done | bytes 5152 | tf_op jit(solution)/shard_map/ppermute | solution.py:17
  53.3 1.7 %maximum_maximum_fusion.1 = (bf16[2,10,321,128]{3,2,1,0:T(8,128)(2,1)S(1)}, bf16[2,10,321,128]{3,2,1,0:T(8,128)(2,1)S(1)}) fusion(bf16[2,1,320,128]{3,2,1,0:T(8,128)(2,1)S(1)} %collective-permute-done.6, bf16[1,8,320,128]{3,2,1,0:T(8,128)(2,1)S(1)} %multiply_convert_fusion.1, bf16[1,8,320,128]{3,2,1,0:T(8,128)(2,1)S(1)} %copy-done.3, ...), kind=kLoop, calls=%fused_computation.113 | loop fusion | flops 16435200 | bytes 4935680 | tf_op jit(solution)/shard_map/concatenate | solution.py:13
  55.0 0.7 %fusion.116 = (bf16[1,8,320,128]{3,2,1,0:T(8,128)(2,1)S(1)}, bf16[1,8,320,128]{3,2,1,0:T(8,128)(2,1)S(1)}, bf16[1,8,320,128]{3,2,1,0:T(8,128)(2,1)S(1)}, bf16[1,...) fusion(bf16[2,10,321,128]{3,2,1,0:T(8,128)(2,1)S(1)} %get-tuple-element.30), kind=kLoop, calls=%fused_computation.188 | loop fusion | bytes 7864320 | tf_op jit(solution)/shard_map/slice | solution.py:46
  55.7 0.9 %fusion.115 = (bf16[1,8,320,128]{3,2,1,0:T(8,128)(2,1)S(1)}, bf16[1,8,320,128]{3,2,1,0:T(8,128)(2,1)S(1)}, bf16[1,8,320,128]{3,2,1,0:T(8,128)(2,1)S(1)}, bf16[1,...) fusion(bf16[2,10,321,128]{3,2,1,0:T(8,128)(2,1)S(1)} %get-tuple-element.29), kind=kLoop, calls=%fused_computation.187 | loop fusion | bytes 7864320 | tf_op jit(solution)/shard_map/slice | solution.py:46
  56.6 0.6 pad_maximum_fusion.3
  57.4 1.0 %copy-done.6 = bf16[3,3,3,128,128]{4,3,2,1,0:T(8,128)(2,1)S(1)} copy-done((bf16[3,3,3,128,128]{4,3,2,1,0:T(8,128)(2,1)S(1)}, bf16[3,3,3,128,128]{4,3,2,1,0:T(8,128)(2,1)}, u32[]{:S(2)}) %copy-start.6) | copy-done | bytes 884760
  58.4 0.7 %fusion.48 = f32[2560,128]{1,0:T(8,128)S(1)} fusion(bf16[2560,128]{1,0:T(8,128)(2,1)S(1)} %bitcast.172, bf16[2560,128]{1,0:T(8,128)(2,1)S(1)} %bitcast.168, bf16[2560,128]{1,0:T(8,128)(2,1)S(1)} %bitcast.175, bf16[3,3,384,128]{3,2,1,0:T(8,128)(2,1)S(1)} %bitcast.197), kind=kOutput, calls=%fused_computation.64 | convolution fusion | flops 257556480 | bytes 3375104 | tf_op jit(solution)/shard_map/dot_general | solution.py:53
  59.0 0.7 %convolution_add_fusion.7 = f32[2560,128]{1,0:T(8,128)S(1)} fusion(f32[2560,128]{1,0:T(8,128)S(1)} %fusion.48, bf16[2560,128]{1,0:T(8,128)(2,1)S(1)} %bitcast.171, bf16[2560,128]{1,0:T(8,128)(2,1)S(1)} %bitcast.133, bf16[2560,128]{1,0:T(8,128)(2,1)S(1)} %bitcast.174, bf16[3,3,384,128]{3,2,1,0:T(8,128)(2,1)S(1)} %bitcast.198), kind=kOutput, calls=%fused_computation.7 | convolution fusion | flops 257884160 | bytes 4685824 | tf_op jit(solution)/shard_map/dot_general | solution.py:53
  59.7 0.7 %convolution_add_fusion.6 = f32[2560,128]{1,0:T(8,128)S(1)} fusion(f32[2560,128]{1,0:T(8,128)S(1)} %convolution_add_fusion.7, bf16[2560,128]{1,0:T(8,128)(2,1)S(1)} %bitcast.170, bf16[2560,128]{1,0:T(8,128)(2,1)S(1)} %bitcast.166, bf16[2560,128]{1,0:T(8,128)(2,1)S(1)} %bitcast.173, bf16[3,3,384,128]{3,2,1,0:T(8,128)(2,1)S(1)} %bitcast.199), kind=kOutput, calls=%fused_computation.6 | convolution fusion | flops 257884160 | bytes 4685824 | tf_op jit(solution)/shard_map/dot_general | solution.py:53
  60.4 1.1 %fusion.119 = (bf16[1,8,320,128]{3,2,1,0:T(8,128)(2,1)S(1)}, bf16[1,8,320,128]{3,2,1,0:T(8,128)(2,1)S(1)}, bf16[1,8,320,128]{3,2,1,0:T(8,128)(2,1)S(1)}, bf16[1,...) fusion(bf16[1,10,322,128]{3,2,1,0:T(8,128)(2,1)S(1)} %bitcast.128), kind=kLoop, calls=%fused_computation.191 | loop fusion | bytes 11796480 | tf_op jit(solution)/shard_map/slice | solution.py:46
  61.6 0.7 %convolution_add_fusion.5 = f32[2560,128]{1,0:T(8,128)S(1)} fusion(f32[2560,128]{1,0:T(8,128)S(1)} %convolution_add_fusion.6, bf16[2560,128]{1,0:T(8,128)(2,1)S(1)} %bitcast.152, bf16[2560,128]{1,0:T(8,128)(2,1)S(1)} %bitcast.153, bf16[2560,128]{1,0:T(8,128)(2,1)S(1)} %bitcast.154, bf16[3,3,384,128]{3,2,1,0:T(8,128)(2,1)S(1)} %bitcast.200), kind=kOutput, calls=%fused_computation.5 | convolution fusion | flops 257884160 | bytes 4685824 | tf_op jit(solution)/shard_map/dot_general | solution.py:53
  62.2 0.7 %convolution_add_fusion.4 = f32[2560,128]{1,0:T(8,128)S(1)} fusion(f32[2560,128]{1,0:T(8,128)S(1)} %convolution_add_fusion.5, bf16[2560,128]{1,0:T(8,128)(2,1)S(1)} %bitcast.146, bf16[2560,128]{1,0:T(8,128)(2,1)S(1)} %bitcast.147, bf16[2560,128]{1,0:T(8,128)(2,1)S(1)} %bitcast.148, bf16[3,3,384,128]{3,2,1,0:T(8,128)(2,1)S(1)} %bitcast.201), kind=kOutput, calls=%fused_computation.4 | convolution fusion | flops 257884160 | bytes 4685824 | tf_op jit(solution)/shard_map/dot_general | solution.py:53
  62.9 0.7 %convolution_add_fusion.3 = f32[2560,128]{1,0:T(8,128)S(1)} fusion(f32[2560,128]{1,0:T(8,128)S(1)} %convolution_add_fusion.4, bf16[2560,128]{1,0:T(8,128)(2,1)S(1)} %bitcast.141, bf16[2560,128]{1,0:T(8,128)(2,1)S(1)} %bitcast.142, bf16[2560,128]{1,0:T(8,128)(2,1)S(1)} %bitcast.140, bf16[3,3,384,128]{3,2,1,0:T(8,128)(2,1)S(1)} %bitcast.202), kind=kOutput, calls=%fused_computation.3 | convolution fusion | flops 257884160 | bytes 4685824 | tf_op jit(solution)/shard_map/dot_general | solution.py:53
  63.6 0.7 %convolution_add_fusion.2 = f32[2560,128]{1,0:T(8,128)S(1)} fusion(f32[2560,128]{1,0:T(8,128)S(1)} %convolution_add_fusion.3, bf16[2560,128]{1,0:T(8,128)(2,1)S(1)} %bitcast.163, bf16[2560,128]{1,0:T(8,128)(2,1)S(1)} %bitcast.158, bf16[2560,128]{1,0:T(8,128)(2,1)S(1)} %bitcast.165, bf16[3,3,384,128]{3,2,1,0:T(8,128)(2,1)S(1)} %bitcast.203), kind=kOutput, calls=%fused_computation.2 | convolution fusion | flops 257884160 | bytes 4685824 | tf_op jit(solution)/shard_map/dot_general | solution.py:53
  64.3 0.7 %convolution_add_fusion.1 = f32[2560,128]{1,0:T(8,128)S(1)} fusion(f32[2560,128]{1,0:T(8,128)S(1)} %convolution_add_fusion.2, bf16[2560,128]{1,0:T(8,128)(2,1)S(1)} %bitcast.161, bf16[2560,128]{1,0:T(8,128)(2,1)S(1)} %get-tuple-element.71, bf16[2560,128]{1,0:T(8,128)(2,1)S(1)} %bitcast.164, bf16[3,3,384,128]{3,2,1,0:T(8,128)(2,1)S(1)} %bitcast.204), kind=kOutput, calls=%fused_computation.1 | convolution fusion | flops 257884160 | bytes 4685824 | tf_op jit(solution)/shard_map/dot_general | solution.py:53
  65.0 0.7 %fusion.1 = f32[2560,128]{1,0:T(8,128)S(1)} fusion(f32[2560,128]{1,0:T(8,128)S(1)} %convolution_add_fusion.1, bf16[2560,128]{1,0:T(8,128)(2,1)S(1)} %bitcast.160, bf16[2560,128]{1,0:T(8,128)(2,1)S(1)} %bitcast.156, bf16[2560,128]{1,0:T(8,128)(2,1)S(1)} %bitcast.162, f32[128]{0:T(128)S(1)} %copy-done.8, bf16[3,3,384,128]{3,2,1,0:T(8,128)(2,1)S(1)} %bitcast.205), kind=kOutput, calls=%fused_computation.17 | convolution fusion | flops 258211840 | bytes 4686336 | tf_op jit(solution)/shard_map/dot_general | solution.py:53
  65.7 1.0 %add_convert_fusion = bf16[1,8,320,128]{3,2,1,0:T(8,128)(2,1)} fusion(f32[1,8,320,128]{3,2,1,0:T(8,128)S(1)} %bitcast.131, f32[1,8,320,128]{3,2,1,0:T(8,128)S(1)} %bitcast.135), kind=kLoop, calls=%fused_computation.116 | loop fusion | flops 655360 | bytes 3276800 | tf_op jit(solution)/shard_map/convert_element_type | solution.py:78
  (32 shorter events, 2.5 us)
Async XLA Ops:
  0.0 1.0 %copy-start = (bf16[1,4,160,256]{3,2,1,0:T(8,128)(2,1)S(1)}, bf16[1,4,160,256]{3,2,1,0:T(8,128)(2,1)}, u32[]{:S(2)}) copy-start(bf16[1,4,160,256]{3,2,1,0:T(8,128)(2,1)} %param.9) | copy-start | bytes 983044
  2.1 1.1 %copy-start.2 = (bf16[1,8,320,128]{3,2,1,0:T(8,128)(2,1)S(1)}, bf16[1,8,320,128]{3,2,1,0:T(8,128)(2,1)}, u32[]{:S(2)}) copy-start(bf16[1,8,320,128]{3,2,1,0:T(8,128)(2,1)} %param.12) | copy-start | bytes 1966084
  3.2 9.1 %collective-permute-start.1 = (bf16[2,1,320,128]{3,2,1,0:T(8,128)(2,1)S(1)}, bf16[2,1,320,128]{3,2,1,0:T(8,128)(2,1)S(1)}, u32[]{:S(2)}, u32[]{:S(2)}) collective-permute-start(bf16[2,1,320,128]{3,2,1,0:T(8,128)(2,1)S(1)} %get-tuple-element.52), channel_id=1, source_target_pairs={{4,0},{8,4},{12,8},{5,1},{9,5},{13,9},{6,2},{10,6},{14,10},{7,3},{... | collective-permute-start | bytes 491528 | tf_op jit(solution)/shard_map/ppermute | solution.py:17
  4.5 9.0 %collective-permute-start = (bf16[2,1,320,128]{3,2,1,0:T(8,128)(2,1)S(1)}, bf16[2,1,320,128]{3,2,1,0:T(8,128)(2,1)S(1)}, u32[]{:S(2)}, u32[]{:S(2)}) collective-permute-start(bf16[2,1,320,128]{3,2,1,0:T(8,128)(2,1)S(1)} %get-tuple-element.51), channel_id=1, source_target_pairs={{0,4},{4,8},{8,12},{1,5},{5,9},{9,13},{2,6},{6,10},{10,14},{3,7},{... | collective-permute-start | bytes 491528 | tf_op jit(solution)/shard_map/ppermute | solution.py:15
  13.6 5.2 %collective-permute-start.2 = (bf16[2,10,1,128]{3,2,1,0:T(2,128)(2,1)S(1)}, bf16[2,10,1,128]{3,2,1,0:T(2,128)(2,1)S(1)}, u32[]{:S(2)}, u32[]{:S(2)}) collective-permute-start(bf16[2,10,1,128]{3,2,1,0:T(2,128)(2,1)S(1)} %get-tuple-element.35), channel_id=1, source_target_pairs={{0,2},{1,3},{4,6},{5,7},{8,10},{9,11},{12,14},{13,15},{16,18},{17,... | collective-permute-start | bytes 15368 | tf_op jit(solution)/shard_map/ppermute | solution.py:15
  17.2 5.6 %collective-permute-start.3 = (bf16[2,10,1,128]{3,2,1,0:T(2,128)(2,1)S(1)}, bf16[2,10,1,128]{3,2,1,0:T(2,128)(2,1)S(1)}, u32[]{:S(2)}, u32[]{:S(2)}) collective-permute-start(bf16[2,10,1,128]{3,2,1,0:T(2,128)(2,1)S(1)} %get-tuple-element.36), channel_id=1, source_target_pairs={{2,0},{3,1},{6,4},{7,5},{10,8},{11,9},{14,12},{15,13},{18,16},{19,... | collective-permute-start | bytes 15368 | tf_op jit(solution)/shard_map/ppermute | solution.py:17
  23.4 5.4 %collective-permute-start.4 = (bf16[10,322,128]{2,1,0:T(8,128)(2,1)S(1)}, bf16[10,322,128]{2,1,0:T(8,128)(2,1)S(1)}, u32[]{:S(2)}, u32[]{:S(2)}) collective-permute-start(bf16[10,322,128]{2,1,0:T(8,128)(2,1)S(1)} %fusion.96), channel_id=1, source_target_pairs={{0,1},{1,0},{2,3},{3,2},{4,5},{5,4},{6,7},{7,6},{8,9},{9,8},{10,11... | collective-permute-start | bytes 2472968 | tf_op jit(solution)/shard_map/ppermute | solution.py:25
  25.2 1.5 %copy-start.5 = (bf16[3,3,3,128,128]{4,3,2,1,0:T(8,128)(2,1)S(1)}, bf16[3,3,3,128,128]{4,3,2,1,0:T(8,128)(2,1)}, u32[]{:S(2)}) copy-start(bf16[3,3,3,128,128]{4,3,2,1,0:T(8,128)(2,1)} %param.14) | copy-start | bytes 2654212
  31.9 1.1 %copy-start.4 = (bf16[2560,128]{1,0:T(8,128)(2,1)S(1)}, bf16[2560,128]{1,0:T(8,128)(2,1)}, u32[]{:S(2)}) copy-start(bf16[2560,128]{1,0:T(8,128)(2,1)} %multiply_convert_fusion.2) | copy-start | bytes 1966084
  33.0 0.7 %copy-start.7 = (f32[128]{0:T(128)S(1)}, f32[128]{0:T(128)}, u32[]{:S(2)}) copy-start(f32[128]{0:T(128)} %param.15) | copy-start | bytes 1540
  34.5 1.1 %copy-start.3 = (bf16[1,8,320,128]{3,2,1,0:T(8,128)(2,1)S(1)}, bf16[1,8,320,128]{3,2,1,0:T(8,128)(2,1)}, u32[]{:S(2)}) copy-start(bf16[1,8,320,128]{3,2,1,0:T(8,128)(2,1)} %param.13) | copy-start | bytes 1966084
  35.6 9.2 %collective-permute-start.6 = (bf16[2,1,320,128]{3,2,1,0:T(8,128)(2,1)S(1)}, bf16[2,1,320,128]{3,2,1,0:T(8,128)(2,1)S(1)}, u32[]{:S(2)}, u32[]{:S(2)}) collective-permute-start(bf16[2,1,320,128]{3,2,1,0:T(8,128)(2,1)S(1)} %get-tuple-element.48), channel_id=1, source_target_pairs={{4,0},{8,4},{12,8},{5,1},{9,5},{13,9},{6,2},{10,6},{14,10},{7,3},{... | collective-permute-start | bytes 491528 | tf_op jit(solution)/shard_map/ppermute | solution.py:17
  36.9 9.1 %collective-permute-start.5 = (bf16[2,1,320,128]{3,2,1,0:T(8,128)(2,1)S(1)}, bf16[2,1,320,128]{3,2,1,0:T(8,128)(2,1)S(1)}, u32[]{:S(2)}, u32[]{:S(2)}) collective-permute-start(bf16[2,1,320,128]{3,2,1,0:T(8,128)(2,1)S(1)} %get-tuple-element.47), channel_id=1, source_target_pairs={{0,4},{4,8},{8,12},{1,5},{5,9},{9,13},{2,6},{6,10},{10,14},{3,7},{... | collective-permute-start | bytes 491528 | tf_op jit(solution)/shard_map/ppermute | solution.py:15
  46.1 3.5 %collective-permute-start.7 = (bf16[2,10,1,128]{3,2,1,0:T(2,128)(2,1)S(1)}, bf16[2,10,1,128]{3,2,1,0:T(2,128)(2,1)S(1)}, u32[]{:S(2)}, u32[]{:S(2)}) collective-permute-start(bf16[2,10,1,128]{3,2,1,0:T(2,128)(2,1)S(1)} %get-tuple-element.31), channel_id=1, source_target_pairs={{0,2},{1,3},{4,6},{5,7},{8,10},{9,11},{12,14},{13,15},{16,18},{17,... | collective-permute-start | bytes 15368 | tf_op jit(solution)/shard_map/ppermute | solution.py:15
  47.7 5.6 %collective-permute-start.8 = (bf16[2,10,1,128]{3,2,1,0:T(2,128)(2,1)S(1)}, bf16[2,10,1,128]{3,2,1,0:T(2,128)(2,1)S(1)}, u32[]{:S(2)}, u32[]{:S(2)}) collective-permute-start(bf16[2,10,1,128]{3,2,1,0:T(2,128)(2,1)S(1)} %get-tuple-element.32), channel_id=1, source_target_pairs={{2,0},{3,1},{6,4},{7,5},{10,8},{11,9},{14,12},{15,13},{18,16},{19,... | collective-permute-start | bytes 15368 | tf_op jit(solution)/shard_map/ppermute | solution.py:17
  57.2 1.2 %copy-start.6 = (bf16[3,3,3,128,128]{4,3,2,1,0:T(8,128)(2,1)S(1)}, bf16[3,3,3,128,128]{4,3,2,1,0:T(8,128)(2,1)}, u32[]{:S(2)}) copy-start(bf16[3,3,3,128,128]{4,3,2,1,0:T(8,128)(2,1)} %param.16) | copy-start | bytes 2654212
  57.3 3.1 %collective-permute-start.9 = (bf16[10,322,128]{2,1,0:T(8,128)(2,1)S(1)}, bf16[10,322,128]{2,1,0:T(8,128)(2,1)S(1)}, u32[]{:S(2)}, u32[]{:S(2)}) collective-permute-start(bf16[10,322,128]{2,1,0:T(8,128)(2,1)S(1)} %fusion.95), channel_id=1, source_target_pairs={{0,1},{1,0},{2,3},{3,2},{4,5},{5,4},{6,7},{7,6},{8,9},{9,8},{10,11... | collective-permute-start | bytes 2472968 | tf_op jit(solution)/shard_map/ppermute | solution.py:25
  64.3 0.7 %copy-start.8 = (f32[128]{0:T(128)S(1)}, f32[128]{0:T(128)}, u32[]{:S(2)}) copy-start(f32[128]{0:T(128)} %param.17) | copy-start | bytes 1540
  65.0 1.7 %copy-start.1 = (bf16[1,4,160,256]{3,2,1,0:T(8,128)(2,1)S(1)}, bf16[1,4,160,256]{3,2,1,0:T(8,128)(2,1)}, u32[]{:S(2)}) copy-start(bf16[1,4,160,256]{3,2,1,0:T(8,128)(2,1)} %param.9) | copy-start | bytes 983044
where the time goes:
time: 67.2 us; the launch traced here: 66.7 us
  starting transfers between devices  21.3 us (32%)
  waiting for transfers between devices  14 us (21%)
  matrix products  13.4 us (20%)
  local copies, waits for them, and re-layouts  9.14 us (14%)
  other arithmetic  8.4 us (12%)
    ppermute x4, starting transfers between devices, padded_2(): lax.ppermute(tail, axis, [(i, (i + 1) % count) for i in range(ends)])  15.8 us
    dot_general x18, matrix products, causal_conv(): jnp.dot(stencil, folded[frame_step, row_step], preferred_element_type=jnp...  12.3 us
    ppermute x4, waiting for transfers between devices, padded_2(): lax.ppermute(head, axis, [((i + 1) % count, i) for i in range(ends)])  11.6 us
    ppermute x4, starting transfers between devices, padded_2(): lax.ppermute(head, axis, [((i + 1) % count, i) for i in range(ends)])  5.35 us
    slice x5, local copies, waits for them, and re-layouts, causal_conv(): padded[frame_step, row_step:row_step + tile_rows, col_step:col_step + til...  5.26 us
    concatenate x6, other arithmetic, padded_2(): jnp.concatenate([lax.ppermute(tail, axis, [(i, (i + 1) % count) for i in...  5.23 us
    unnamed x18, local copies, waits for them, and re-layouts  3.38 us
    ppermute x4, waiting for transfers between devices, padded_2(): lax.ppermute(tail, axis, [(i, (i + 1) % count) for i in range(ends)])  2.37 us
  transfers between devices with their start and end apart: 10, of which 6 were waited for; matrix products, arithmetic and copies ran while one was open for 14% of the time, Pallas kernels for 0%

commit v1 on v0

v1 whole, which is shorter than its diff:
```python
import functools

import jax
import jax.numpy as jnp
from jax import lax
from jax.experimental import pallas as pl
from jax.experimental.pallas import tpu as pltpu
from jax.sharding import PartitionSpec as P

EDGE = 16
STEP = 2
MESH = pl.DeviceIdType.MESH
SIDES = [(-1, 0), (1, 0), (0, -1), (0, 1), (-1, -1), (-1, 1), (1, -1), (1, 1)]


def kernel(rows_n, cols_n, lat_h, pw_h, pb, c1_h, c2_h, w1_h, b1, w2_h, b2, out_h,
           lat, pw, w, F, L, up, obuf, s1, s2,
           load_sem, send_sem, recv_sem, mid_send, mid_recv, out_sem):
    R, W = c1_h.shape[1], c1_h.shape[2]
    CH = c1_h.shape[3]
    WP = W + EDGE
    HR, HW = lat.shape[0], lat.shape[1]
    blocks = R // STEP
    r, c, f = lax.axis_index("row"), lax.axis_index("col"), lax.axis_index("frm")
    caches = (c1_h, c2_h)
    up_ok, down_ok = r > 0, r < rows_n - 1
    left_ok, right_ok = c > 0, c < cols_n - 1

    def exists(d):
        dr, dc = SIDES[d]
        ok = None
        for test in ([up_ok] if dr < 0 else [down_ok] if dr > 0 else []) + (
                [left_ok] if dc < 0 else [right_ok] if dc > 0 else []):
            ok = test if ok is None else jnp.logical_and(ok, test)
        return ok

    def where_is(d):
        dr, dc = SIDES[d]
        ids = {}
        if dr:
            ids["row"] = r + dr
        if dc:
            ids["col"] = c + dc
        return ids

    loads = []

    def load(src, dst):
        cp = pltpu.make_async_copy(src, dst, load_sem.at[len(loads)])
        cp.start()
        loads.append(cp)
        return cp

    lat_cp = load(lat_h.at[0], lat)
    pw_cp = load(pw_h, pw)
    cache_cp = [load(caches[0].at[0], F.at[0, 0, pl.ds(1, R), pl.ds(0, W)])]
    w_cp = [[load(w1_h.at[:, :, q], w.at[0, :, :, :, pl.ds(q * CH, CH)]) for q in range(3)]]
    cache_cp.append(load(caches[1].at[0], F.at[1, 0, pl.ds(1, R), pl.ds(0, W)]))
    w_cp.append([load(w2_h.at[:, :, q], w.at[1, :, :, :, pl.ds(q * CH, CH)]) for q in range(3)])

    barrier = pltpu.get_barrier_semaphore()
    for d in range(8):
        @pl.when(exists(d))
        def _():
            pl.semaphore_signal(barrier, inc=1, device_id=where_is(d), device_id_type=MESH)
    pl.semaphore_signal(barrier, inc=1, device_id={"frm": 1 - f}, device_id_type=MESH)
    tall = 1 + up_ok.astype(jnp.int32) + down_ok.astype(jnp.int32)
    wide = 1 + left_ok.astype(jnp.int32) + right_ok.astype(jnp.int32)
    pl.semaphore_wait(barrier, tall * wide)

    def side_copy(cv, which, d, from_hbm=False):
        dr, dc = SIDES[d]
        row = 0 if dr < 0 else R - 1
        land_row = R + 1 if dr < 0 else 0
        col = pl.ds(0, EDGE) if dc < 0 else pl.ds(W - EDGE, EDGE)
        side = 1 if dc < 0 else 0
        fr = 2 * which
        if dc == 0:
            rs, cs = pl.ds(row, 1), pl.ds(0, W)
            dst = F.at[cv, fr, pl.ds(land_row, 1), pl.ds(0, W)]
        elif dr == 0:
            rs, cs = pl.ds(0, R), col
            dst = L.at[cv, which, side, pl.ds(1, R)]
        else:
            rs, cs = pl.ds(row, 1), col
            dst = L.at[cv, which, side, pl.ds(land_row, 1)]
        if from_hbm:
            src = caches[cv].at[0, rs, cs]
        else:
            src = F.at[cv, fr, pl.ds(1 + rs.start, rs.size), cs]
        return pltpu.make_async_remote_copy(
            src_ref=src, dst_ref=dst, send_sem=send_sem.at[cv, which, d],
            recv_sem=recv_sem.at[cv, which, d], device_id=where_is(d), device_id_type=MESH)

    def send_sides(cv, which, ds, from_hbm=False):
        for d in ds:
            @pl.when(exists(d))
            def _():
                side_copy(cv, which, d, from_hbm).start()

    def recv_sides(cv, which, ds):
        for d in ds:
            opposite = SIDES.index((-SIDES[d][0], -SIDES[d][1]))

            @pl.when(exists(opposite))
            def _():
                side_copy(cv, which, d, which == 0).wait_recv()

    def drain_sides(cv, which):
        for d in range(8):
            @pl.when(exists(d))
            def _():
                side_copy(cv, which, d, which == 0).wait_send()

    partner = {"frm": 1 - f}

    def main_copy(cv, i, cache):
        here = pl.ds(1 + i * STEP, STEP)
        if cache:
            src = caches[cv].at[0, pl.ds(i * STEP, STEP)]
        else:
            src = F.at[cv, 2, here, pl.ds(0, W)]
        return pltpu.make_async_remote_copy(
            src_ref=src, dst_ref=F.at[cv, 1, here, pl.ds(0, W)], send_sem=mid_send.at[cv, i],
            recv_sem=mid_recv.at[cv, i], device_id=partner, device_id_type=MESH)

    payload = 2 * (1 - f)

    def rim_copy(cv, part):
        if part < 2:
            rs, cs = pl.ds((R + 1) * part, 1), pl.ds(0, WP)
        else:
            rs, cs = pl.ds(1, R), pl.ds(W, EDGE)
        return pltpu.make_async_remote_copy(
            src_ref=F.at[cv, payload, rs, cs], dst_ref=F.at[cv, 1, rs, cs],
            send_sem=mid_send.at[cv, blocks + part], recv_sem=mid_recv.at[cv, blocks + part],
            device_id=partner, device_id_type=MESH)

    def merge(cv, which):
        left, right = L[cv, which, 0], L[cv, which, 1]
        place = lax.broadcasted_iota(jnp.int32, left.shape, 1)
        tile = jnp.where(place < EDGE // 2, right.astype(jnp.float32), left.astype(jnp.float32))
        F[cv, 2 * which, :, pl.ds(W, EDGE)] = tile.astype(jnp.bfloat16)

    send_sides(0, 0, range(8), True)

    @pl.when(f == 1)
    def _():
        for i in range(blocks):
            main_copy(0, i, True).start()

    for cv in range(2):
        for which in range(2):
            for ok, row in ((up_ok, 0), (down_ok, R + 1)):
                @pl.when(jnp.logical_not(ok))
                def _():
                    F[cv, 2 * which, row, pl.ds(0, W)] = jnp.zeros((W, CH), jnp.bfloat16)

                for side, across in ((0, left_ok), (1, right_ok)):
                    @pl.when(jnp.logical_not(jnp.logical_and(ok, across)))
                    def _():
                        L[cv, which, side, row] = jnp.zeros((EDGE, CH), jnp.bfloat16)
            for side, across in ((0, left_ok), (1, right_ok)):
                @pl.when(jnp.logical_not(across))
                def _():
                    L[cv, which, side, pl.ds(1, R)] = jnp.zeros((R, EDGE, CH), jnp.bfloat16)

    lat_cp.wait()
    pw_cp.wait()

    def project(i, carry):
        v = jnp.dot(lat[i], pw[...], preferred_element_type=jnp.float32) + pb[...]
        v = v.astype(jnp.bfloat16).astype(jnp.float32)
        a = v / (1.0 + jnp.exp(-v))
        for k in range(2):
            s1[pl.ds(k, HW, stride=2), :] = v
            s2[pl.ds(k, HW, stride=2), :] = a
        up[i] = s1[...].astype(jnp.bfloat16)
        wide = s2[...].astype(jnp.bfloat16)
        F[0, 2, 1 + 2 * i, pl.ds(0, W)] = wide
        F[0, 2, 2 + 2 * i, pl.ds(0, W)] = wide
        return carry

    lax.fori_loop(0, HR, project, 0)
    send_sides(0, 1, range(8))

    @pl.when(f == 0)
    def _():
        for i in range(blocks):
            main_copy(0, i, False).start()

    send_sides(1, 0, range(8), True)

    @pl.when(f == 1)
    def _():
        for i in range(blocks):
            main_copy(1, i, True).start()

    def taps(cv, first, count, base):
        lhs = jnp.concatenate(
            [F[cv, a, pl.ds(base + p, STEP)].reshape(STEP * WP, CH)
             for a in range(first, first + count) for p in range(3)], axis=1)
        rhs = w[cv, pl.ds(first, count)].reshape(count * 3 * CH, 3 * CH)
        return jnp.dot(lhs, rhs, preferred_element_type=jnp.float32)

    def fold(z, n):
        z = z[n * WP:(n + 1) * WP]
        return (pltpu.roll(z[:, :CH], 1, 0)[:W] + z[:W, CH:2 * CH]
                + pltpu.roll(z[:, 2 * CH:], WP - 1, 0)[:W])

    def arrive(cv):
        recv_sides(cv, 0, range(8))
        merge(cv, 0)
        recv_sides(cv, 1, range(8))
        merge(cv, 1)
        for part in range(3):
            rim_copy(cv, part).start()
        for i in range(blocks):
            main_copy(cv, i, False).wait_recv()
        for part in range(3):
            rim_copy(cv, part).wait_recv()

    cache_cp[0].wait()
    for cp in w_cp[0]:
        cp.wait()
    arrive(0)

    def first(k, carry):
        i = lax.rem(k + blocks - 1, blocks)
        base = i * STEP
        z = taps(0, 0, 3, base)
        for n in range(STEP):
            y = fold(z, n) + b1[...]
            F[1, 2, base + n + 1, pl.ds(0, W)] = (y / (1.0 + jnp.exp(-y))).astype(jnp.bfloat16)

        @pl.when(k == 1)
        def _():
            send_sides(1, 1, (0, 1, 4, 5, 6, 7))

        @pl.when(f == 0)
        def _():
            main_copy(1, i, False).start()
        return carry

    lax.fori_loop(0, blocks, first, 0)
    send_sides(1, 1, (2, 3))
    cache_cp[1].wait()
    for cp in w_cp[1]:
        cp.wait()
    arrive(1)

    def second(k, carry):
        i = lax.rem(k + 1, blocks)
        base = i * STEP
        z = taps(1, 0, 3, base)
        for n in range(STEP):
            y = fold(z, n) + b2[...] + up[(base + n) // 2].astype(jnp.float32)
            obuf[base + n] = y.astype(jnp.bfloat16)
        pltpu.make_async_copy(obuf.at[pl.ds(base, STEP)], out_h.at[0, pl.ds(base, STEP)],
                              out_sem.at[i]).start()
        return carry

    lax.fori_loop(0, blocks, second, 0)
    for cv in range(2):
        for which in range(2):
            drain_sides(cv, which)
        for i in range(blocks):
            main_copy(cv, i, False).wait_send()
        for part in range(3):
            rim_copy(cv, part).wait_send()
    for i in range(blocks):
        pltpu.make_async_copy(obuf.at[pl.ds(i * STEP, STEP)], out_h.at[0, pl.ds(i * STEP, STEP)],
                              out_sem.at[i]).wait()


def per_device(latent, proj_weight, proj_bias, cache_one, cache_two,
               conv_one, bias_one, conv_two, bias_two):
    _, R, W, CH = cache_one.shape
    _, HR, HW, LCH = latent.shape
    blocks = R // STEP
    WP = W + EDGE
    anywhere = pl.BlockSpec(memory_space=pl.ANY)
    vmem = pl.BlockSpec(memory_space=pltpu.VMEM)
    bf = jnp.bfloat16
    return pl.pallas_call(
        functools.partial(kernel, lax.axis_size("row"), lax.axis_size("col")),
        out_shape=jax.ShapeDtypeStruct(cache_one.shape, bf),
        in_specs=[anywhere, anywhere, vmem, anywhere, anywhere, anywhere, vmem, anywhere, vmem],
        out_specs=anywhere,
        scratch_shapes=[
            pltpu.VMEM((HR, HW, LCH), bf),
            pltpu.VMEM((LCH, CH), bf),
            pltpu.VMEM((2, 3, 3, CH, 3 * CH), bf),
            pltpu.VMEM((2, 3, R + 2, WP, CH), bf),
            pltpu.VMEM((2, 2, 2, R + 2, EDGE, CH), bf),
            pltpu.VMEM((HR, W, CH), bf),
            pltpu.VMEM((R, W, CH), bf),
            pltpu.VMEM((W, CH), jnp.float32),
            pltpu.VMEM((W, CH), jnp.float32),
            pltpu.SemaphoreType.DMA((10,)),
            pltpu.SemaphoreType.DMA((2, 2, 8)),
            pltpu.SemaphoreType.DMA((2, 2, 8)),
            pltpu.SemaphoreType.DMA((2, blocks + 3)),
            pltpu.SemaphoreType.DMA((2, blocks + 3)),
            pltpu.SemaphoreType.DMA((blocks,)),
        ],
        compiler_params=pltpu.CompilerParams(
            collective_id=0, has_side_effects=True, vmem_limit_bytes=60 * 1024 * 1024),
        name="decoder_window",
    )(latent, proj_weight, proj_bias.reshape(1, CH), cache_one, cache_two,
      conv_one, bias_one.reshape(1, CH), conv_two, bias_two.reshape(1, CH))


def solution(mesh):
    placed = P(("grp", "frm"), "row", "col", None)
    return jax.shard_map(
        per_device,
        mesh=mesh,
        in_specs=(placed, P(), P(), placed, placed, P(), P(), P(), P()),
        out_specs=placed,
        check_vma=False,
    )
```

time: 67.2 us -> 28.5 us (0.42)
  Pallas kernels: 0 us -> 26.4 us
  starting transfers between devices: 21.3 us -> 0 us
  waiting for transfers between devices: 14 us -> 0 us
  matrix products: 13.4 us -> 0 us
  other arithmetic: 8.4 us -> 0 us
  local copies, waits for them, and re-layouts: 9.14 us -> 1.97 us
    pallas_call x0 -> x1, Pallas kernels: none -> 26.4 us  [per_device(): pl.pallas_call(functools.partial(kernel, lax.axis_size('row'), lax.axis_s...]
    ppermute x10 -> x0, starting transfers between devices: 21.3 us -> none  [the longest x4 15.8 us: padded_2(): lax.ppermute(tail, axis, [(i, (i + 1) % count) for i in range(ends)])]
    ppermute x10 -> x0, waiting for transfers between devices: 14 us -> none  [the longest x4 11.6 us: padded_2(): lax.ppermute(head, axis, [((i + 1) % count, i) for i in range(ends)])]
    dot_general x19 -> x0, matrix products: 13.4 us -> none  [the longest x18 12.3 us: causal_conv(): jnp.dot(stencil, folded[frame_step, row_step], preferred_element_type=jnp...]
    slice x5 -> x0, local copies, waits for them, and re-layouts: 5.26 us -> none  [causal_conv(): padded[frame_step, row_step:row_step + tile_rows, col_step:col_step + til...]
    concatenate x6 -> x0, other arithmetic: 5.23 us -> none  [padded_2(): jnp.concatenate([lax.ppermute(tail, axis, [(i, (i + 1) % count) for i in...]
    convert_element_type x4 -> x0, other arithmetic: 2.91 us -> none  [the longest x2 1.54 us: per_device(): act_one = jax.nn.silu(upsampled.astype(jnp.float32)).astype(jnp.bfloat16)]
    unnamed x18 -> x1, local copies, waits for them, and re-layouts: 3.38 us -> 1.97 us
  transfers between devices with their start and end apart: 10 -> 0, of which waited for: 6 -> 0; matrix products, arithmetic and copies ran while one was open for 14% -> 0% of each run, Pallas kernels for 0% -> 0%
where the time goes in v1:
time: 28.5 us; the launch traced here: 28.4 us
  Pallas kernels  26.4 us (93%)
  local copies, waits for them, and re-layouts  1.97 us (7%)
    pallas_call x1, Pallas kernels, per_device(): pl.pallas_call(functools.partial(kernel, lax.axis_size('row'), lax.axis_s...  26.4 us
    unnamed x1, local copies, waits for them, and re-layouts  1.97 us

profile of v1, /device:TPU:0, one launch (start us, length us, event | category | flops | bytes accessed | tf_op | source)
XLA Modules:
  0.0 28.4 jit_solution(12788506646725748443)
XLA Ops:
  0.0 26.4 %decoder_window.1 = bf16[1,8,320,128]{3,2,1,0:T(8,128)(2,1)} custom-call(bf16[1,4,160,256]{3,2,1,0:T(8,128)(2,1)} %lat_h.1, bf16[256,128]{1,0:T(8,128)(2,1)} %pw_h.1, f32[1,128]{1,0:T(1,128)} %bitcast.3, bf16[1,8,320,128]{3,2,1,0:T(8,128)(2,1)} %c1_h.1, bf16[1,8,320,128]{3,2,1,0:T(8,128)(2,1)} %c2_h.1, bf16[3,3,3,128,128]{4,3,2,1,0:T(8,128)(2,1)} %w1_h.1, ...), custom_call_target="tpu_custom_call" | custom-call | tf_op jit(solution)/shard_map/decoder_window/pallas_call | solution.py:285
  26.4 2.0 %copy.11 = bf16[1,8,320,128]{3,2,1,0:T(8,128)(2,1)} copy(bf16[1,8,320,128]{3,2,1,0:T(8,128)(2,1)} %decoder_window.1) | data formatting | bytes 1310720

commit v2 on v1

--- a/solution.py
+++ b/solution.py
@@ -14,7 +14,7 @@
 
 
 def kernel(rows_n, cols_n, lat_h, pw_h, pb, c1_h, c2_h, w1_h, b1, w2_h, b2, out_h,
-           lat, pw, w, F, L, up, obuf, s1, s2,
+           lat, pw, w, F, L, up, obuf, acc, s1, s2,
            load_sem, send_sem, recv_sem, mid_send, mid_recv, out_sem):
     R, W = c1_h.shape[1], c1_h.shape[2]
     CH = c1_h.shape[3]
@@ -136,11 +136,11 @@
             send_sem=mid_send.at[cv, blocks + part], recv_sem=mid_recv.at[cv, blocks + part],
             device_id=partner, device_id_type=MESH)
 
-    def merge(cv, which):
-        left, right = L[cv, which, 0], L[cv, which, 1]
+    def merge(cv, which, rs):
+        left, right = L[cv, which, 0, rs], L[cv, which, 1, rs]
         place = lax.broadcasted_iota(jnp.int32, left.shape, 1)
         tile = jnp.where(place < EDGE // 2, right.astype(jnp.float32), left.astype(jnp.float32))
-        F[cv, 2 * which, :, pl.ds(W, EDGE)] = tile.astype(jnp.bfloat16)
+        F[cv, 2 * which, rs, pl.ds(W, EDGE)] = tile.astype(jnp.bfloat16)
 
     send_sides(0, 0, range(8), True)
 
@@ -196,11 +196,11 @@
         for i in range(blocks):
             main_copy(1, i, True).start()
 
-    def taps(cv, first, count, base):
+    def taps(cv, frames, base):
         lhs = jnp.concatenate(
             [F[cv, a, pl.ds(base + p, STEP)].reshape(STEP * WP, CH)
-             for a in range(first, first + count) for p in range(3)], axis=1)
-        rhs = w[cv, pl.ds(first, count)].reshape(count * 3 * CH, 3 * CH)
+             for a in frames for p in range(3)], axis=1)
+        rhs = jnp.concatenate([w[cv, a].reshape(3 * CH, 3 * CH) for a in frames], axis=0)
         return jnp.dot(lhs, rhs, preferred_element_type=jnp.float32)
 
     def fold(z, n):
@@ -208,59 +208,110 @@
         return (pltpu.roll(z[:, :CH], 1, 0)[:W] + z[:W, CH:2 * CH]
                 + pltpu.roll(z[:, 2 * CH:], WP - 1, 0)[:W])
 
-    def arrive(cv):
-        recv_sides(cv, 0, range(8))
-        merge(cv, 0)
-        recv_sides(cv, 1, range(8))
-        merge(cv, 1)
-        for part in range(3):
-            rim_copy(cv, part).start()
-        for i in range(blocks):
-            main_copy(cv, i, False).wait_recv()
-        for part in range(3):
-            rim_copy(cv, part).wait_recv()
+    def begin(cv, frames, i):
+        z = taps(cv, frames, i * STEP)
+        for n in range(STEP):
+            acc[i * STEP + n] = fold(z, n)
+
+    def finish_one(i):
+        base = i * STEP
+        z = taps(0, (1,), base)
+        for n in range(STEP):
+            y = fold(z, n) + acc[base + n] + b1[...]
+            F[1, 2, base + n + 1, pl.ds(0, W)] = (y / (1.0 + jnp.exp(-y))).astype(jnp.bfloat16)
+
+        @pl.when(f == 0)
+        def _():
+            main_copy(1, i, False).start()
+
+    def out_copy(i):
+        here = pl.ds(i * STEP, STEP)
+        return pltpu.make_async_copy(obuf.at[here], out_h.at[0, here], out_sem.at[i])
+
+    def finish_two(i):
+        base = i * STEP
+        z = taps(1, (1, 2), base)
+        for n in range(STEP):
+            y = fold(z, n) + acc[base + n] + b2[...] + up[(base + n) // 2].astype(jnp.float32)
+            obuf[base + n] = y.astype(jnp.bfloat16)
+        out_copy(i).start()
+
+    def each(body, start, count):
+        def step(k, carry):
+            body(lax.rem(start + k, blocks))
+            return carry
+
+        lax.fori_loop(0, count, step, 0)
+
+    def inner(body):
+        each(body, 1, blocks - 2)
+
+    def outer(body):
+        each(body, blocks - 1, 2)
+
+    cols, tall_ds = (2, 3), (0, 1, 4, 5, 6, 7)
+    body_rows, rims = pl.ds(1, R), (pl.ds(0, 1), pl.ds(R + 1, 1))
 
     cache_cp[0].wait()
     for cp in w_cp[0]:
         cp.wait()
-    arrive(0)
-
-    def first(k, carry):
-        i = lax.rem(k + blocks - 1, blocks)
-        base = i * STEP
-        z = taps(0, 0, 3, base)
-        for n in range(STEP):
-            y = fold(z, n) + b1[...]
-            F[1, 2, base + n + 1, pl.ds(0, W)] = (y / (1.0 + jnp.exp(-y))).astype(jnp.bfloat16)
-
-        @pl.when(k == 1)
-        def _():
-            send_sides(1, 1, (0, 1, 4, 5, 6, 7))
-
-        @pl.when(f == 0)
-        def _():
-            main_copy(1, i, False).start()
-        return carry
-
-    lax.fori_loop(0, blocks, first, 0)
-    send_sides(1, 1, (2, 3))
+    for which in range(2):
+        recv_sides(0, which, cols)
+        merge(0, which, body_rows)
+    rim_copy(0, 2).start()
+    inner(lambda i: begin(0, (0, 2), i))
+    for which in range(2):
+        recv_sides(0, which, tall_ds)
+        for rs in rims:
+            merge(0, which, rs)
+    for part in range(2):
+        rim_copy(0, part).start()
+    outer(lambda i: begin(0, (0, 2), i))
+    for i in range(blocks):
+        main_copy(0, i, False).wait_recv()
+    for part in range(3):
+        rim_copy(0, part).wait_recv()
+    outer(finish_one)
+    send_sides(1, 1, tall_ds)
+    inner(finish_one)
+    send_sides(1, 1, cols)
+
     cache_cp[1].wait()
     for cp in w_cp[1]:
         cp.wait()
-    arrive(1)
-
-    def second(k, carry):
-        i = lax.rem(k + 1, blocks)
-        base = i * STEP
-        z = taps(1, 0, 3, base)
-        for n in range(STEP):
-            y = fold(z, n) + b2[...] + up[(base + n) // 2].astype(jnp.float32)
-            obuf[base + n] = y.astype(jnp.bfloat16)
-        pltpu.make_async_copy(obuf.at[pl.ds(base, STEP)], out_h.at[0, pl.ds(base, STEP)],
-                              out_sem.at[i]).start()
-        return carry
-
-    lax.fori_loop(0, blocks, second, 0)
+    recv_sides(1, 0, range(8))
+    merge(1, 0, pl.ds(0, R + 2))
+
+    @pl.when(f == 1)
+    def _():
+        for part in range(3):
+            rim_copy(1, part).start()
+
+    each(lambda i: begin(1, (0,), i), 0, blocks)
+    recv_sides(1, 1, cols)
+    merge(1, 1, body_rows)
+
+    @pl.when(f == 0)
+    def _():
+        rim_copy(1, 2).start()
+
+    for i in range(blocks):
+        main_copy(1, i, False).wait_recv()
+    rim_copy(1, 2).wait_recv()
+    inner(finish_two)
+    recv_sides(1, 1, tall_ds)
+    for rs in rims:
+        merge(1, 1, rs)
+
+    @pl.when(f == 0)
+    def _():
+        for part in range(2):
+            rim_copy(1, part).start()
+
+    for part in range(2):
+        rim_copy(1, part).wait_recv()
+    outer(finish_two)
+
     for cv in range(2):
         for which in range(2):
             drain_sides(cv, which)
@@ -269,8 +320,7 @@
         for part in range(3):
             rim_copy(cv, part).wait_send()
     for i in range(blocks):
-        pltpu.make_async_copy(obuf.at[pl.ds(i * STEP, STEP)], out_h.at[0, pl.ds(i * STEP, STEP)],
-                              out_sem.at[i]).wait()
+        out_copy(i).wait()
 
 
 def per_device(latent, proj_weight, proj_bias, cache_one, cache_two,
@@ -295,6 +345,7 @@
             pltpu.VMEM((2, 2, 2, R + 2, EDGE, CH), bf),
             pltpu.VMEM((HR, W, CH), bf),
             pltpu.VMEM((R, W, CH), bf),
+            pltpu.VMEM((R, W, CH), jnp.float32),
             pltpu.VMEM((W, CH), jnp.float32),
             pltpu.VMEM((W, CH), jnp.float32),
             pltpu.SemaphoreType.DMA((10,)),

time: 28.5 us -> 26.1 us (0.916)
  the two profiles are of different devices: /device:TPU:0 before, /device:TPU:1 now
where the time goes in v2:
time: 26.1 us; the launch traced here: 25.9 us
  Pallas kernels  23.9 us (92%)
  local copies, waits for them, and re-layouts  1.97 us (8%)
    pallas_call x1, Pallas kernels, per_device(): pl.pallas_call(functools.partial(kernel, lax.axis_size('row'), lax.axis_s...  23.9 us
    unnamed x1, local copies, waits for them, and re-layouts  1.97 us

profile of v2, /device:TPU:1, one launch (start us, length us, event | category | flops | bytes accessed | tf_op | source)
XLA Modules:
  0.0 25.9 jit_solution(10570041893299709352)
XLA Ops:
  0.0 23.9 %decoder_window.1 = bf16[1,8,320,128]{3,2,1,0:T(8,128)(2,1)} custom-call(bf16[1,4,160,256]{3,2,1,0:T(8,128)(2,1)} %lat_h.1, bf16[256,128]{1,0:T(8,128)(2,1)} %pw_h.1, f32[1,128]{1,0:T(1,128)} %bitcast.3, bf16[1,8,320,128]{3,2,1,0:T(8,128)(2,1)} %c1_h.1, bf16[1,8,320,128]{3,2,1,0:T(8,128)(2,1)} %c2_h.1, bf16[3,3,3,128,128]{4,3,2,1,0:T(8,128)(2,1)} %w1_h.1, ...), custom_call_target="tpu_custom_call" | custom-call | tf_op jit(solution)/shard_map/decoder_window/pallas_call | solution.py:335
  23.9 2.0 %copy.11 = bf16[1,8,320,128]{3,2,1,0:T(8,128)(2,1)} copy(bf16[1,8,320,128]{3,2,1,0:T(8,128)(2,1)} %decoder_window.1) | data formatting | bytes 1310720

commit v3 on v2

--- a/solution.py
+++ b/solution.py
@@ -14,11 +14,10 @@
 
 
 def kernel(rows_n, cols_n, lat_h, pw_h, pb, c1_h, c2_h, w1_h, b1, w2_h, b2, out_h,
-           lat, pw, w, F, L, up, obuf, acc, s1, s2,
+           lat, pw, w, F, S, L, up, obuf, acc, s1, s2,
            load_sem, send_sem, recv_sem, mid_send, mid_recv, out_sem):
     R, W = c1_h.shape[1], c1_h.shape[2]
     CH = c1_h.shape[3]
-    WP = W + EDGE
     HR, HW = lat.shape[0], lat.shape[1]
     blocks = R // STEP
     r, c, f = lax.axis_index("row"), lax.axis_index("col"), lax.axis_index("frm")
@@ -128,19 +127,19 @@
 
     def rim_copy(cv, part):
         if part < 2:
-            rs, cs = pl.ds((R + 1) * part, 1), pl.ds(0, WP)
+            src, dst = (F.at[cv, fr, pl.ds((R + 1) * part, 1)] for fr in (payload, 1))
         else:
-            rs, cs = pl.ds(1, R), pl.ds(W, EDGE)
+            src, dst = (S.at[cv, fr] for fr in (payload, 1))
         return pltpu.make_async_remote_copy(
-            src_ref=F.at[cv, payload, rs, cs], dst_ref=F.at[cv, 1, rs, cs],
+            src_ref=src, dst_ref=dst,
             send_sem=mid_send.at[cv, blocks + part], recv_sem=mid_recv.at[cv, blocks + part],
             device_id=partner, device_id_type=MESH)
 
-    def merge(cv, which, rs):
-        left, right = L[cv, which, 0, rs], L[cv, which, 1, rs]
+    def merge(cv, which):
+        left, right = L[cv, which, 0], L[cv, which, 1]
         place = lax.broadcasted_iota(jnp.int32, left.shape, 1)
         tile = jnp.where(place < EDGE // 2, right.astype(jnp.float32), left.astype(jnp.float32))
-        F[cv, 2 * which, rs, pl.ds(W, EDGE)] = tile.astype(jnp.bfloat16)
+        S[cv, 2 * which] = tile.astype(jnp.bfloat16)
 
     send_sides(0, 0, range(8), True)
 
@@ -196,29 +195,53 @@
         for i in range(blocks):
             main_copy(1, i, True).start()
 
-    def taps(cv, frames, base):
+    def weights(cv, frames):
+        return jnp.concatenate([w[cv, a].reshape(3 * CH, 3 * CH) for a in frames], axis=0)
+
+    def taps(cv, frames, i):
         lhs = jnp.concatenate(
-            [F[cv, a, pl.ds(base + p, STEP)].reshape(STEP * WP, CH)
+            [F[cv, a, pl.ds(i * STEP + p, STEP)].reshape(STEP * W, CH)
              for a in frames for p in range(3)], axis=1)
-        rhs = jnp.concatenate([w[cv, a].reshape(3 * CH, 3 * CH) for a in frames], axis=0)
-        return jnp.dot(lhs, rhs, preferred_element_type=jnp.float32)
+        return jnp.dot(lhs, weights(cv, frames), preferred_element_type=jnp.float32)
+
+    spot = lax.broadcasted_iota(jnp.int32, (8, CH), 0)
 
     def fold(z, n):
-        z = z[n * WP:(n + 1) * WP]
-        return (pltpu.roll(z[:, :CH], 1, 0)[:W] + z[:W, CH:2 * CH]
-                + pltpu.roll(z[:, 2 * CH:], WP - 1, 0)[:W])
-
-    def begin(cv, frames, i):
-        z = taps(cv, frames, i * STEP)
+        z = z[n * W:(n + 1) * W]
+        after = pltpu.roll(z[:, :CH], 1, 0)
+        after = jnp.concatenate([jnp.where(spot == 0, 0.0, after[:8]), after[8:]], axis=0)
+        ahead = pltpu.roll(z[:, 2 * CH:], W - 1, 0)
+        ahead = jnp.concatenate([ahead[:W - 8], jnp.where(spot == 7, 0.0, ahead[W - 8:])], axis=0)
+        return after + z[:, CH:2 * CH] + ahead
+
+    def begin(cv, frames):
+        def body(i):
+            z = taps(cv, frames, i)
+            for n in range(STEP):
+                acc[i * STEP + n] = fold(z, n)
+        return body
+
+    def more(cv, frames):
+        def body(i):
+            z = taps(cv, frames, i)
+            for n in range(STEP):
+                acc[i * STEP + n] += fold(z, n)
+        return body
+
+    def sides(cv):
+        lhs = jnp.concatenate(
+            [S[cv, a, pl.ds(p, R)].reshape(R * EDGE, CH) for a in range(3) for p in range(3)],
+            axis=1)
+        z = jnp.dot(lhs, weights(cv, range(3)), preferred_element_type=jnp.float32)
+        for n in range(R):
+            part = z[n * EDGE:(n + 1) * EDGE]
+            acc[n, pl.ds(0, 1)] += part[EDGE - 1:, :CH]
+            acc[n, pl.ds(W - 1, 1)] += part[:1, 2 * CH:]
+
+    def finish_one(i):
         for n in range(STEP):
-            acc[i * STEP + n] = fold(z, n)
-
-    def finish_one(i):
-        base = i * STEP
-        z = taps(0, (1,), base)
-        for n in range(STEP):
-            y = fold(z, n) + acc[base + n] + b1[...]
-            F[1, 2, base + n + 1, pl.ds(0, W)] = (y / (1.0 + jnp.exp(-y))).astype(jnp.bfloat16)
+            y = acc[i * STEP + n] + b1[...]
+            F[1, 2, i * STEP + n + 1] = (y / (1.0 + jnp.exp(-y))).astype(jnp.bfloat16)
 
         @pl.when(f == 0)
         def _():
@@ -230,9 +253,8 @@
 
     def finish_two(i):
         base = i * STEP
-        z = taps(1, (1, 2), base)
         for n in range(STEP):
-            y = fold(z, n) + acc[base + n] + b2[...] + up[(base + n) // 2].astype(jnp.float32)
+            y = acc[base + n] + b2[...] + up[(base + n) // 2].astype(jnp.float32)
             obuf[base + n] = y.astype(jnp.bfloat16)
         out_copy(i).start()
 
@@ -250,27 +272,27 @@
         each(body, blocks - 1, 2)
 
     cols, tall_ds = (2, 3), (0, 1, 4, 5, 6, 7)
-    body_rows, rims = pl.ds(1, R), (pl.ds(0, 1), pl.ds(R + 1, 1))
+
+    def mids(cv):
+        for i in range(blocks):
+            main_copy(cv, i, False).wait_recv()
 
     cache_cp[0].wait()
     for cp in w_cp[0]:
         cp.wait()
+    inner(begin(0, (0, 2)))
+    mids(0)
+    inner(more(0, (1,)))
     for which in range(2):
-        recv_sides(0, which, cols)
-        merge(0, which, body_rows)
-    rim_copy(0, 2).start()
-    inner(lambda i: begin(0, (0, 2), i))
-    for which in range(2):
-        recv_sides(0, which, tall_ds)
-        for rs in rims:
-            merge(0, which, rs)
-    for part in range(2):
+        recv_sides(0, which, range(8))
+        merge(0, which)
+    for part in range(3):
         rim_copy(0, part).start()
-    outer(lambda i: begin(0, (0, 2), i))
-    for i in range(blocks):
-        main_copy(0, i, False).wait_recv()
+    outer(begin(0, (0, 2)))
     for part in range(3):
         rim_copy(0, part).wait_recv()
+    outer(more(0, (1,)))
+    sides(0)
     outer(finish_one)
     send_sides(1, 1, tall_ds)
     inner(finish_one)
@@ -280,36 +302,30 @@
     for cp in w_cp[1]:
         cp.wait()
     recv_sides(1, 0, range(8))
-    merge(1, 0, pl.ds(0, R + 2))
+    merge(1, 0)
 
     @pl.when(f == 1)
     def _():
         for part in range(3):
             rim_copy(1, part).start()
 
-    each(lambda i: begin(1, (0,), i), 0, blocks)
-    recv_sides(1, 1, cols)
-    merge(1, 1, body_rows)
+    each(begin(1, (0,)), 0, blocks)
+    mids(1)
+    inner(more(1, (1, 2)))
+    recv_sides(1, 1, range(8))
+    merge(1, 1)
 
     @pl.when(f == 0)
     def _():
-        rim_copy(1, 2).start()
-
-    for i in range(blocks):
-        main_copy(1, i, False).wait_recv()
-    rim_copy(1, 2).wait_recv()
+        for part in range(3):
+            rim_copy(1, part).start()
+
+    outer(more(1, (2,)))
+    for part in range(3):
+        rim_copy(1, part).wait_recv()
+    sides(1)
     inner(finish_two)
-    recv_sides(1, 1, tall_ds)
-    for rs in rims:
-        merge(1, 1, rs)
-
-    @pl.when(f == 0)
-    def _():
-        for part in range(2):
-            rim_copy(1, part).start()
-
-    for part in range(2):
-        rim_copy(1, part).wait_recv()
+    outer(more(1, (1,)))
     outer(finish_two)
 
     for cv in range(2):
@@ -328,7 +344,6 @@
     _, R, W, CH = cache_one.shape
     _, HR, HW, LCH = latent.shape
     blocks = R // STEP
-    WP = W + EDGE
     anywhere = pl.BlockSpec(memory_space=pl.ANY)
     vmem = pl.BlockSpec(memory_space=pltpu.VMEM)
     bf = jnp.bfloat16
@@ -341,7 +356,8 @@
             pltpu.VMEM((HR, HW, LCH), bf),
             pltpu.VMEM((LCH, CH), bf),
             pltpu.VMEM((2, 3, 3, CH, 3 * CH), bf),
-            pltpu.VMEM((2, 3, R + 2, WP, CH), bf),
+            pltpu.VMEM((2, 3, R + 2, W, CH), bf),
+            pltpu.VMEM((2, 3, R + 2, EDGE, CH), bf),
             pltpu.VMEM((2, 2, 2, R + 2, EDGE, CH), bf),
             pltpu.VMEM((HR, W, CH), bf),
             pltpu.VMEM((R, W, CH), bf),

time: 26.1 us -> 25.7 us (0.985)
  the two profiles are of different devices: /device:TPU:1 before, /device:TPU:0 now
where the time goes in v3:
time: 25.7 us; the launch traced here: 25.5 us
  Pallas kernels  23.5 us (91%)
  local copies, waits for them, and re-layouts  1.97 us (8%)
    pallas_call x1, Pallas kernels, per_device(): pl.pallas_call(functools.partial(kernel, lax.axis_size('row'), lax.axis_s...  23.5 us
    unnamed x1, local copies, waits for them, and re-layouts  1.97 us

profile of v3, /device:TPU:0, one launch (start us, length us, event | category | flops | bytes accessed | tf_op | source)
XLA Modules:
  0.0 25.5 jit_solution(9687997733050798724)
XLA Ops:
  0.0 23.5 %decoder_window.1 = bf16[1,8,320,128]{3,2,1,0:T(8,128)(2,1)} custom-call(bf16[1,4,160,256]{3,2,1,0:T(8,128)(2,1)} %lat_h.1, bf16[256,128]{1,0:T(8,128)(2,1)} %pw_h.1, f32[1,128]{1,0:T(1,128)} %bitcast.3, bf16[1,8,320,128]{3,2,1,0:T(8,128)(2,1)} %c1_h.1, bf16[1,8,320,128]{3,2,1,0:T(8,128)(2,1)} %c2_h.1, bf16[3,3,3,128,128]{4,3,2,1,0:T(8,128)(2,1)} %w1_h.1, ...), custom_call_target="tpu_custom_call" | custom-call | tf_op jit(solution)/shard_map/decoder_window/pallas_call | solution.py:350
  23.5 2.0 %copy.11 = bf16[1,8,320,128]{3,2,1,0:T(8,128)(2,1)} copy(bf16[1,8,320,128]{3,2,1,0:T(8,128)(2,1)} %decoder_window.1) | data formatting | bytes 1310720

commit v4 on v3

--- a/solution.py
+++ b/solution.py
@@ -8,13 +8,13 @@
 from jax.sharding import PartitionSpec as P
 
 EDGE = 16
-STEP = 2
+STEP = 1
 MESH = pl.DeviceIdType.MESH
 SIDES = [(-1, 0), (1, 0), (0, -1), (0, 1), (-1, -1), (-1, 1), (1, -1), (1, 1)]
 
 
 def kernel(rows_n, cols_n, lat_h, pw_h, pb, c1_h, c2_h, w1_h, b1, w2_h, b2, out_h,
-           lat, pw, w, F, S, L, up, obuf, acc, s1, s2,
+           lat, pw, w, F, S, L, up, obuf, acc, ca, CL, s1, s2,
            load_sem, send_sem, recv_sem, mid_send, mid_recv, out_sem):
     R, W = c1_h.shape[1], c1_h.shape[2]
     CH = c1_h.shape[3]
@@ -83,7 +83,10 @@
         else:
             rs, cs = pl.ds(row, 1), col
             dst = L.at[cv, which, side, pl.ds(land_row, 1)]
-        if from_hbm:
+        if cv == 0 and which == 1 and dc == 0:
+            src = ca.at[pl.ds(0 if dr < 0 else HR - 1, 1)]
+            dst = CL.at[pl.ds(1 if dr < 0 else 0, 1)]
+        elif from_hbm:
             src = caches[cv].at[0, rs, cs]
         else:
             src = F.at[cv, fr, pl.ds(1 + rs.start, rs.size), cs]
@@ -171,6 +174,7 @@
         v = jnp.dot(lat[i], pw[...], preferred_element_type=jnp.float32) + pb[...]
         v = v.astype(jnp.bfloat16).astype(jnp.float32)
         a = v / (1.0 + jnp.exp(-v))
+        ca[i] = a.astype(jnp.bfloat16)
         for k in range(2):
             s1[pl.ds(k, HW, stride=2), :] = v
             s2[pl.ds(k, HW, stride=2), :] = a
@@ -283,11 +287,29 @@
     inner(begin(0, (0, 2)))
     mids(0)
     inner(more(0, (1,)))
-    for which in range(2):
-        recv_sides(0, which, range(8))
-        merge(0, which)
-    for part in range(3):
-        rim_copy(0, part).start()
+    recv_sides(0, 0, range(8))
+    merge(0, 0)
+
+    @pl.when(f == 1)
+    def _():
+        for part in range(3):
+            rim_copy(0, part).start()
+
+    recv_sides(0, 1, range(8))
+    merge(0, 1)
+    for k, ok in ((0, up_ok), (1, down_ok)):
+        @pl.when(ok)
+        def _():
+            a = CL[k].astype(jnp.float32)
+            for n in range(2):
+                s2[pl.ds(n, HW, stride=2), :] = a
+            F[0, 2, k * (R + 1)] = s2[...].astype(jnp.bfloat16)
+
+    @pl.when(f == 0)
+    def _():
+        for part in range(3):
+            rim_copy(0, part).start()
+
     outer(begin(0, (0, 2)))
     for part in range(3):
         rim_copy(0, part).wait_recv()
@@ -362,6 +384,8 @@
             pltpu.VMEM((HR, W, CH), bf),
             pltpu.VMEM((R, W, CH), bf),
             pltpu.VMEM((R, W, CH), jnp.float32),
+            pltpu.VMEM((HR, HW, CH), bf),
+            pltpu.VMEM((2, HW, CH), bf),
             pltpu.VMEM((W, CH), jnp.float32),
             pltpu.VMEM((W, CH), jnp.float32),
             pltpu.SemaphoreType.DMA((10,)),

time: 25.7 us -> 24.5 us (0.953)
  Pallas kernels: 23.5 us -> 22 us
    pallas_call x1, Pallas kernels: 23.5 us -> 22 us  [per_device(): pl.pallas_call(functools.partial(kernel, lax.axis_size('row'), lax.axis_s...]
where the time goes in v4:
time: 24.5 us; the launch traced here: 24 us
  Pallas kernels  22 us (90%)
  local copies, waits for them, and re-layouts  1.97 us (8%)
    pallas_call x1, Pallas kernels, per_device(): pl.pallas_call(functools.partial(kernel, lax.axis_size('row'), lax.axis_s...  22 us
    unnamed x1, local copies, waits for them, and re-layouts  1.97 us

profile of v4, /device:TPU:0, one launch (start us, length us, event | category | flops | bytes accessed | tf_op | source)
XLA Modules:
  0.0 24.0 jit_solution(16545976816983592129)
XLA Ops:
  0.0 22.0 %decoder_window.1 = bf16[1,8,320,128]{3,2,1,0:T(8,128)(2,1)} custom-call(bf16[1,4,160,256]{3,2,1,0:T(8,128)(2,1)} %lat_h.1, bf16[256,128]{1,0:T(8,128)(2,1)} %pw_h.1, f32[1,128]{1,0:T(1,128)} %bitcast.3, bf16[1,8,320,128]{3,2,1,0:T(8,128)(2,1)} %c1_h.1, bf16[1,8,320,128]{3,2,1,0:T(8,128)(2,1)} %c2_h.1, bf16[3,3,3,128,128]{4,3,2,1,0:T(8,128)(2,1)} %w1_h.1, ...), custom_call_target="tpu_custom_call" | custom-call | tf_op jit(solution)/shard_map/decoder_window/pallas_call | solution.py:372
  22.0 2.0 %copy.11 = bf16[1,8,320,128]{3,2,1,0:T(8,128)(2,1)} copy(bf16[1,8,320,128]{3,2,1,0:T(8,128)(2,1)} %decoder_window.1) | data formatting | bytes 1310720

commit v5 on v4

--- a/solution.py
+++ b/solution.py
@@ -9,12 +9,14 @@
 
 EDGE = 16
 STEP = 1
+GROUP = 2
 MESH = pl.DeviceIdType.MESH
 SIDES = [(-1, 0), (1, 0), (0, -1), (0, 1), (-1, -1), (-1, 1), (1, -1), (1, 1)]
 
 
-def kernel(rows_n, cols_n, lat_h, pw_h, pb, c1_h, c2_h, w1_h, b1, w2_h, b2, out_h,
-           lat, pw, w, F, S, L, up, obuf, acc, ca, CL, s1, s2,
+def kernel(rows_n, cols_n, lat_h, pw_h, pb_h, c1_h, c2_h, w1_h, b1_h, w2_h, b2_h, out_h,
+
+           lat, pw, w, F, S, L, up, obuf, acc, ca, CL, s1, s2, pb, b1, b2,
            load_sem, send_sem, recv_sem, mid_send, mid_recv, out_sem):
     R, W = c1_h.shape[1], c1_h.shape[2]
     CH = c1_h.shape[3]
@@ -52,6 +54,7 @@
 
     lat_cp = load(lat_h.at[0], lat)
     pw_cp = load(pw_h, pw)
+    bias_cp = [load(src, dst) for src, dst in ((pb_h, pb), (b1_h, b1), (b2_h, b2))]
     cache_cp = [load(caches[0].at[0], F.at[0, 0, pl.ds(1, R), pl.ds(0, W)])]
     w_cp = [[load(w1_h.at[:, :, q], w.at[0, :, :, :, pl.ds(q * CH, CH)]) for q in range(3)]]
     cache_cp.append(load(caches[1].at[0], F.at[1, 0, pl.ds(1, R), pl.ds(0, W)]))
@@ -167,8 +170,8 @@
                 def _():
                     L[cv, which, side, pl.ds(1, R)] = jnp.zeros((R, EDGE, CH), jnp.bfloat16)
 
-    lat_cp.wait()
-    pw_cp.wait()
+    for cp in [lat_cp, pw_cp] + bias_cp:
+        cp.wait()
 
     def project(i, carry):
         v = jnp.dot(lat[i], pw[...], preferred_element_type=jnp.float32) + pb[...]
@@ -202,9 +205,9 @@
     def weights(cv, frames):
         return jnp.concatenate([w[cv, a].reshape(3 * CH, 3 * CH) for a in frames], axis=0)
 
-    def taps(cv, frames, i):
+    def taps(cv, frames, i, size):
         lhs = jnp.concatenate(
-            [F[cv, a, pl.ds(i * STEP + p, STEP)].reshape(STEP * W, CH)
+            [F[cv, a, pl.ds(i + p, size)].reshape(size * W, CH)
              for a in frames for p in range(3)], axis=1)
         return jnp.dot(lhs, weights(cv, frames), preferred_element_type=jnp.float32)
 
@@ -218,18 +221,18 @@
         ahead = jnp.concatenate([ahead[:W - 8], jnp.where(spot == 7, 0.0, ahead[W - 8:])], axis=0)
         return after + z[:, CH:2 * CH] + ahead
 
-    def begin(cv, frames):
+    def begin(cv, frames, size=1):
         def body(i):
-            z = taps(cv, frames, i)
-            for n in range(STEP):
-                acc[i * STEP + n] = fold(z, n)
+            z = taps(cv, frames, i, size)
+            for n in range(size):
+                acc[i + n] = fold(z, n)
         return body
 
-    def more(cv, frames):
+    def more(cv, frames, size=1):
         def body(i):
-            z = taps(cv, frames, i)
-            for n in range(STEP):
-                acc[i * STEP + n] += fold(z, n)
+            z = taps(cv, frames, i, size)
+            for n in range(size):
+                acc[i + n] += fold(z, n)
         return body
 
     def sides(cv):
@@ -272,6 +275,17 @@
     def inner(body):
         each(body, 1, blocks - 2)
 
+    group = max(n for n in (1, 2, GROUP) if (R - 2) % n == 0)
+
+    def inner_dots(make, cv, frames):
+        body = make(cv, frames, group)
+
+        def step(k, carry):
+            body(1 + k * group)
+            return carry
+
+        lax.fori_loop(0, (R - 2) // group, step, 0)
+
     def outer(body):
         each(body, blocks - 1, 2)
 
@@ -284,9 +298,9 @@
     cache_cp[0].wait()
     for cp in w_cp[0]:
         cp.wait()
-    inner(begin(0, (0, 2)))
+    inner_dots(begin, 0, (0, 2))
     mids(0)
-    inner(more(0, (1,)))
+    inner_dots(more, 0, (1,))
     recv_sides(0, 0, range(8))
     merge(0, 0)
 
@@ -331,9 +345,10 @@
         for part in range(3):
             rim_copy(1, part).start()
 
-    each(begin(1, (0,)), 0, blocks)
+    inner_dots(begin, 1, (0,))
+    outer(begin(1, (0,)))
     mids(1)
-    inner(more(1, (1, 2)))
+    inner_dots(more, 1, (1, 2))
     recv_sides(1, 1, range(8))
     merge(1, 1)
 
@@ -367,12 +382,11 @@
     _, HR, HW, LCH = latent.shape
     blocks = R // STEP
     anywhere = pl.BlockSpec(memory_space=pl.ANY)
-    vmem = pl.BlockSpec(memory_space=pltpu.VMEM)
     bf = jnp.bfloat16
     return pl.pallas_call(
         functools.partial(kernel, lax.axis_size("row"), lax.axis_size("col")),
         out_shape=jax.ShapeDtypeStruct(cache_one.shape, bf),
-        in_specs=[anywhere, anywhere, vmem, anywhere, anywhere, anywhere, vmem, anywhere, vmem],
+        in_specs=[anywhere] * 9,
         out_specs=anywhere,
         scratch_shapes=[
             pltpu.VMEM((HR, HW, LCH), bf),
@@ -388,7 +402,10 @@
             pltpu.VMEM((2, HW, CH), bf),
             pltpu.VMEM((W, CH), jnp.float32),
             pltpu.VMEM((W, CH), jnp.float32),
-            pltpu.SemaphoreType.DMA((10,)),
+            pltpu.VMEM((1, CH), jnp.float32),
+            pltpu.VMEM((1, CH), jnp.float32),
+            pltpu.VMEM((1, CH), jnp.float32),
+            pltpu.SemaphoreType.DMA((13,)),
             pltpu.SemaphoreType.DMA((2, 2, 8)),
             pltpu.SemaphoreType.DMA((2, 2, 8)),
             pltpu.SemaphoreType.DMA((2, blocks + 3)),

time: 24.5 us -> 23.8 us (0.971)
  Pallas kernels: 22 us -> 21.4 us
    pallas_call x1, Pallas kernels: 22 us -> 21.4 us  [per_device(): pl.pallas_call(functools.partial(kernel, lax.axis_size('row'), lax.axis_s...]
where the time goes in v5:
time: 23.8 us; the launch traced here: 23.4 us
  Pallas kernels  21.4 us (90%)
  local copies, waits for them, and re-layouts  1.97 us (8%)
    pallas_call x1, Pallas kernels, per_device(): pl.pallas_call(functools.partial(kernel, lax.axis_size('row'), lax.axis_s...  21.4 us
    unnamed x1, local copies, waits for them, and re-layouts  1.97 us

profile of v5, /device:TPU:0, one launch (start us, length us, event | category | flops | bytes accessed | tf_op | source)
XLA Modules:
  0.0 23.4 jit_solution(6215724650933108186)
XLA Ops:
  0.0 21.4 %decoder_window.1 = bf16[1,8,320,128]{3,2,1,0:T(8,128)(2,1)} custom-call(bf16[1,4,160,256]{3,2,1,0:T(8,128)(2,1)} %lat_h.1, bf16[256,128]{1,0:T(8,128)(2,1)} %pw_h.1, f32[1,128]{1,0:T(1,128)} %bitcast.3, bf16[1,8,320,128]{3,2,1,0:T(8,128)(2,1)} %c1_h.1, bf16[1,8,320,128]{3,2,1,0:T(8,128)(2,1)} %c2_h.1, bf16[3,3,3,128,128]{4,3,2,1,0:T(8,128)(2,1)} %w1_h.1, ...), custom_call_target="tpu_custom_call" | custom-call | tf_op jit(solution)/shard_map/decoder_window/pallas_call | solution.py:386
  21.4 2.0 %copy.11 = bf16[1,8,320,128]{3,2,1,0:T(8,128)(2,1)} copy(bf16[1,8,320,128]{3,2,1,0:T(8,128)(2,1)} %decoder_window.1) | data formatting | bytes 1310720

commit v6 on v5

--- a/solution.py
+++ b/solution.py
@@ -66,6 +66,22 @@
         def _():
             pl.semaphore_signal(barrier, inc=1, device_id=where_is(d), device_id_type=MESH)
     pl.semaphore_signal(barrier, inc=1, device_id={"frm": 1 - f}, device_id_type=MESH)
+    for cv in range(2):
+        for which in range(2):
+            for ok, row in ((up_ok, 0), (down_ok, R + 1)):
+                @pl.when(jnp.logical_not(ok))
+                def _():
+                    F[cv, 2 * which, row, pl.ds(0, W)] = jnp.zeros((W, CH), jnp.bfloat16)
+
+                for side, across in ((0, left_ok), (1, right_ok)):
+                    @pl.when(jnp.logical_not(jnp.logical_and(ok, across)))
+                    def _():
+                        L[cv, which, side, row] = jnp.zeros((EDGE, CH), jnp.bfloat16)
+            for side, across in ((0, left_ok), (1, right_ok)):
+                @pl.when(jnp.logical_not(across))
+                def _():
+                    L[cv, which, side, pl.ds(1, R)] = jnp.zeros((R, EDGE, CH), jnp.bfloat16)
+
     tall = 1 + up_ok.astype(jnp.int32) + down_ok.astype(jnp.int32)
     wide = 1 + left_ok.astype(jnp.int32) + right_ok.astype(jnp.int32)
     pl.semaphore_wait(barrier, tall * wide)
@@ -153,22 +169,6 @@
     def _():
         for i in range(blocks):
             main_copy(0, i, True).start()
-
-    for cv in range(2):
-        for which in range(2):
-            for ok, row in ((up_ok, 0), (down_ok, R + 1)):
-                @pl.when(jnp.logical_not(ok))
-                def _():
-                    F[cv, 2 * which, row, pl.ds(0, W)] = jnp.zeros((W, CH), jnp.bfloat16)
-
-                for side, across in ((0, left_ok), (1, right_ok)):
-                    @pl.when(jnp.logical_not(jnp.logical_and(ok, across)))
-                    def _():
-                        L[cv, which, side, row] = jnp.zeros((EDGE, CH), jnp.bfloat16)
-            for side, across in ((0, left_ok), (1, right_ok)):
-                @pl.when(jnp.logical_not(across))
-                def _():
-                    L[cv, which, side, pl.ds(1, R)] = jnp.zeros((R, EDGE, CH), jnp.bfloat16)
 
     for cp in [lat_cp, pw_cp] + bias_cp:
         cp.wait()

time: 23.8 us -> 23.8 us (level)
  no operation moved by 1% of the time
where the time goes in v6:
time: 23.8 us; the launch traced here: 23.4 us
  Pallas kernels  21.4 us (90%)
  local copies, waits for them, and re-layouts  1.97 us (8%)
    pallas_call x1, Pallas kernels, per_device(): pl.pallas_call(functools.partial(kernel, lax.axis_size('row'), lax.axis_s...  21.4 us
    unnamed x1, local copies, waits for them, and re-layouts  1.97 us

profile of v6, /device:TPU:0, one launch (start us, length us, event | category | flops | bytes accessed | tf_op | source)
XLA Modules:
  0.0 23.4 jit_solution(10887041600750500538)
XLA Ops:
  0.0 21.4 %decoder_window.1 = bf16[1,8,320,128]{3,2,1,0:T(8,128)(2,1)} custom-call(bf16[1,4,160,256]{3,2,1,0:T(8,128)(2,1)} %lat_h.1, bf16[256,128]{1,0:T(8,128)(2,1)} %pw_h.1, f32[1,128]{1,0:T(1,128)} %bitcast.3, bf16[1,8,320,128]{3,2,1,0:T(8,128)(2,1)} %c1_h.1, bf16[1,8,320,128]{3,2,1,0:T(8,128)(2,1)} %c2_h.1, bf16[3,3,3,128,128]{4,3,2,1,0:T(8,128)(2,1)} %w1_h.1, ...), custom_call_target="tpu_custom_call" | custom-call | tf_op jit(solution)/shard_map/decoder_window/pallas_call | solution.py:386
  21.4 2.0 %copy.11 = bf16[1,8,320,128]{3,2,1,0:T(8,128)(2,1)} copy(bf16[1,8,320,128]{3,2,1,0:T(8,128)(2,1)} %decoder_window.1) | data formatting | bytes 1310720
